TPU v7x, 512 devices: a whole 4x8x8 slice. The times are simulated.
512 devices in a mesh: segment: 4 (over x), dp: 128 (over y, z, core).
Axes of the slice: x: 4, y: 8, z: 8, core: 2. Of those that a mesh axis runs over, the one named last changes fastest.
Arguments:
- fwd_in: bfloat16 [2, 4, 128, 16, 32, 256], P(None, 'segment', 'dp'), may hold values from -6 to 6
- bwd_in: bfloat16 [4, 4, 128, 16, 32, 256], P(None, 'segment', 'dp'), may hold values from -6 to 6
- fresh: bfloat16 [2, 128, 16, 32, 256], P(None, 'dp'), may hold values from -6 to 6
- top_cot: bfloat16 [2, 128, 16, 32, 256], P(None, 'dp'), may hold values from -6 to 6
- conv_weight: bfloat16 [4, 256, 9, 256], P('segment', 'dp'), may hold values from -0.125 to 0.125
Outputs:
- fwd_out: bfloat16 [2, 4, 128, 16, 32, 256], P(None, 'segment', 'dp')
- bwd_out: bfloat16 [4, 4, 128, 16, 32, 256], P(None, 'segment', 'dp')
- weight_grad: float32 [4, 256, 9, 256], P('segment', 'dp')
All inputs are finite; a program needn't handle non-finite values.
Results may differ from a plain program's by a relative error of at most 0.0055.
Values may be sent and summed in bfloat16 or wider, within the bound.
A program may use at most 64 MiB of HBM per device.

v0:
```python
import jax
import jax.numpy as jnp
from jax import lax
from jax.sharding import PartitionSpec as P


def from_partner(x, axis, bit):
    return lax.ppermute(x, axis, [(i, i ^ 1 << bit) for i in range(lax.axis_size(axis))])


def passed_along(block, axis, distance):
    devices = range(lax.axis_size(axis))
    route = [(i - distance, i) for i in devices if i - distance in devices]
    return lax.ppermute(block, axis, route)


def border_send(tile, parity):
    return jnp.where(parity == 0, tile[:, -1], tile[:, 0])


def extend_rows(tile, received, parity):
    blank_row = jnp.zeros_like(received)
    above_row = jnp.where(parity == 1, received, blank_row)[:, None]
    below_row = jnp.where(parity == 0, received, blank_row)[:, None]
    stacked = jnp.concatenate([above_row, tile, below_row], axis=1)
    return jnp.pad(stacked, ((0, 0), (0, 0), (1, 1), (0, 0)))


def window_at(extended, row_off, col_off, height, width, amount):
    portion = extended[:, row_off : row_off + height, col_off : col_off + width, :]
    return portion.reshape(-1, amount)


def conv_part(extended, weight_piece, height, width):
    amount = weight_piece.shape[0]
    running = None
    for row_off in range(3):
        for col_off in range(3):
            product_term = jnp.dot(
                window_at(extended, row_off, col_off, height, width, amount),
                weight_piece[:, 3 * row_off + col_off, :],
                preferred_element_type=jnp.float32,
            )
            running = product_term if running is None else running + product_term
    return running


def conv_transposed(cot_ext, weight_piece, height, width):
    channels = cot_ext.shape[3]
    running = None
    for row_off in range(3):
        for col_off in range(3):
            window = cot_ext[
                :, 2 - row_off : 2 - row_off + height, 2 - col_off : 2 - col_off + width, :
            ].reshape(-1, channels)
            product_term = lax.dot_general(
                window,
                weight_piece[:, 3 * row_off + col_off, :],
                (((1,), (1,)), ((), ())),
                preferred_element_type=jnp.float32,
            )
            running = product_term if running is None else running + product_term
    return running


def grad_part(extended, cotangent, amount, height, width):
    cot_flat = cotangent.reshape(-1, cotangent.shape[3])
    listing = []
    for row_off in range(3):
        for col_off in range(3):
            window = window_at(extended, row_off, col_off, height, width, amount)
            listing.append(
                lax.dot_general(
                    window, cot_flat, (((0,), (0,)), ((), ())), preferred_element_type=jnp.float32
                )
            )
    return jnp.stack(listing, axis=1)


def shards(fwd_in, bwd_in, fresh, top_cot, conv_weight):
    parity = lax.axis_index("dp") % 2
    segment_pos = lax.axis_index("segment")
    last_segment = lax.axis_size("segment") - 1
    weight_shard = conv_weight[0]
    height = fwd_in.shape[3]
    width = fwd_in.shape[4]
    channels = fwd_in.shape[5]
    pixels_all = lax.axis_size("dp") * height * width
    full_weight = lax.all_gather(weight_shard, "dp", axis=0, tiled=True)

    def two_convs(ext_fwd, ext_rec):
        return (
            conv_part(ext_fwd, full_weight, height, width),
            conv_part(ext_rec, full_weight, height, width),
        )

    def back_conv(cot_ext):
        return conv_transposed(cot_ext, full_weight, height, width)

    def one_step(stream_pair, back_four):
        first_in = stream_pair[0]
        second_in = stream_pair[1]
        out_first = back_four[0]
        out_second = back_four[1]
        cot_first = back_four[2]
        cot_second = back_four[3]
        received = from_partner(
            (
                border_send(second_in, parity),
                border_send(out_first, parity),
                border_send(cot_second, parity),
            ),
            "dp",
            0,
        )
        ext_fwd = jnp.maximum(extend_rows(second_in, received[0], parity), 0)
        ext_rec = jnp.maximum(extend_rows(out_first, received[1], parity), 0)
        ext_cot = extend_rows(cot_second, received[2], parity)
        branch_fwd, branch_rec = two_convs(ext_fwd, ext_rec)
        tile_shape = first_in.shape
        new_second = (first_in.astype(jnp.float32) + branch_fwd.reshape(tile_shape)).astype(
            jnp.bfloat16
        )
        forward_pair = jnp.stack([second_in, new_second])
        rebuilt = (out_second.astype(jnp.float32) - branch_rec.reshape(tile_shape)).astype(
            jnp.bfloat16
        )
        through = back_conv(ext_cot).reshape(tile_shape)
        cot_rebuilt = (
            cot_first.astype(jnp.float32) + jnp.where(out_first > 0, through, 0.0)
        ).astype(jnp.bfloat16)
        message = jnp.stack([rebuilt, out_first, cot_second, cot_rebuilt])
        return (forward_pair, message, (ext_rec, cot_second))

    forward_one, message_one, first_terms = one_step(fwd_in[:, 0], bwd_in[:, 0])
    arrived_fwd = passed_along(forward_one, "segment", 1)
    arrived_back = passed_along(message_one, "segment", -1)
    pair_two = jnp.where(segment_pos == 0, fresh, arrived_fwd)
    four_two = jnp.where(
        segment_pos == last_segment, jnp.concatenate([forward_one, top_cot], axis=0), arrived_back
    )
    forward_two, message_two, second_terms = one_step(pair_two, four_two)
    shard_rows = weight_shard.shape[0]
    summed = lax.psum(
        grad_part(first_terms[0], first_terms[1], channels, height, width)
        + grad_part(second_terms[0], second_terms[1], channels, height, width),
        "dp",
    )
    owned = lax.dynamic_slice_in_dim(summed, lax.axis_index("dp") * shard_rows, shard_rows, 0)
    weight_grad = (owned * (2.0 * pixels_all) ** (-0.5))[None]
    return (forward_two[:, None], message_two[:, None], weight_grad)


def solution(mesh):
    in_specs = (
        P(None, "segment", "dp", None, None, None),
        P(None, "segment", "dp", None, None, None),
        P(None, "dp", None, None, None),
        P(None, "dp", None, None, None),
        P("segment", "dp", None, None),
    )
    out_specs = (
        P(None, "segment", "dp", None, None, None),
        P(None, "segment", "dp", None, None, None),
        P("segment", "dp", None, None),
    )
    return jax.shard_map(shards, mesh=mesh, in_specs=in_specs, out_specs=out_specs, check_vma=False)
```

profile of v0, /device:TPU:28, one launch (start us, length us, event | category | flops | bytes accessed | tf_op | source)
XLA Modules:
  0.0 387.7 jit_solution(14345244486883992187)
XLA Ops:
  7.2 1.4 copy.35
  8.7 1.8 slice_bitcast_fusion.4
  10.5 1.9 collective-permute-start
  12.5 1.0 slice_bitcast_fusion.3
  13.4 2.4 collective-permute-start.3
  15.9 1.9 collective-permute-start.4
  18.9 0.8 pad_maximum_fusion.4
  19.7 1.0 fusion.18
  20.7 1.0 fusion.17
  22.0 1.0 fusion.16
  23.0 1.0 fusion.15
  23.9 1.0 fusion.14
  24.9 1.0 fusion.13
  25.9 1.0 fusion.12
  26.9 1.0 fusion.11
  27.9 1.0 fusion.10
  28.9 1.2 fusion.45
  30.0 1.5 fusion.47
  31.5 67.2 %all-gather.3.cloned.1.call-done = bf16[1,256,9,256]{3,2,0,1:T(8,128)(2,1)} async-done(((bf16[1,2,9,256]{3,2,0,1:T(8,128)(2,1)}), bf16[1,256,9,256]{3,2,0,1:T(8,128)(2,1)}) %all-gather.3.cloned.1.call-update) | async-done | bytes 1179664 | tf_op jit(solution)/shard_map/all_gather | solution.py:89
  98.7 2.0 copy.51
  101.2 0.6 copy-done.17
  110.6 3.2 collective-permute-start.1
  114.9 0.7 copy-done.6
  115.8 10.8 %collective-permute-done.1 = bf16[2,1,16,32,256]{4,3,2,1,0:T(8,128)(2,1)S(1)} collective-permute-done((bf16[2,1,16,32,256]{4,3,2,1,0:T(8,128)(2,1)S(1)}, bf16[2,1,16,32,256]{4,3,2,1,0:T(8,128)(2,1)S(1)}, u32[]{:S(2)}, u32[]{:S(2)}) %collective-permute-start.1) | collective-permute-done | bytes 524320 | tf_op jit(solution)/shard_map/ppermute | solution.py:14
  126.8 1.9 collective-permute-start.2
  128.9 2.5 collective-permute-start.5
  134.1 0.8 maximum_bitcast_fusion.1
  134.9 21.4 %collective-permute-done.5 = bf16[4,1,16,32,256]{4,3,2,0,1:T(8,128)(2,1)S(1)} collective-permute-done((bf16[4,1,16,32,256]{4,3,2,0,1:T(8,128)(2,1)S(1)}, bf16[4,1,16,32,256]{4,3,2,0,1:T(8,128)(2,1)S(1)}, u32[]{:S(2)}, u32[]{:S(2)}) %collective-permute-start.5) | collective-permute-done | bytes 1048608 | tf_op jit(solution)/shard_map/ppermute | solution.py:14
  156.5 0.7 slice_bitcast_fusion.1
  157.2 1.9 collective-permute-start.7
  159.2 2.6 collective-permute-start.6
  161.9 1.1 fusion.43
  163.6 0.9 pad_maximum_fusion.2
  166.0 1.1 convolution_add_fusion.13
  167.4 1.1 convolution_add_fusion.12
  168.8 1.1 convolution_add_fusion.11
  170.2 1.1 convolution_add_fusion.10
  171.7 1.1 convolution_add_fusion.9
  173.1 1.1 convolution_add_fusion.8
  174.5 1.9 convolution_add_fusion.7
  176.7 3.4 add.257
  180.1 1.2 copy-done.1
  181.4 1.3 convolution_add_fusion.6
  183.5 0.7 copy-done.8
  185.7 0.7 copy-done.28
  186.5 1.1 maximum_bitcast_fusion
  187.6 191.8 %all-reduce.8.cloned.1.call-done = f32[256,9,256]{2,0,1:T(8,128)} async-done(((f32[256,9,256]{2,0,1:T(8,128)}), f32[256,9,256]{2,0,1:T(8,128)}) %all-reduce.8.cloned.1.call-update) | async-done | bytes 2359312 | tf_op jit(solution)/shard_map/psum | solution.py:144
  379.4 1.5 multiply_bitcast_fusion
  (157 shorter events, 21.3 us)
Async XLA Ops:
  7.2 5.3 %copy-start.5 = (bf16[4,1,1,16,32,256]{5,4,3,2,1,0:T(8,128)(2,1)S(1)}, bf16[4,1,1,16,32,256]{5,4,3,2,1,0:T(8,128)(2,1)}, u32[]{:S(2)}) copy-start(bf16[4,1,1,16,32,256]{5,4,3,2,1,0:T(8,128)(2,1)} %param.6) | copy-start | bytes 3145732
  7.2 91.5 %all-gather.3.cloned.1.call-start = ((), (), s32[]{:S(2)}) async-start(), calls=%async_computation.1 | async-start | bytes 2113536 | tf_op jit(solution)/shard_map/all_gather | solution.py:89
  8.6 370.7 %all-reduce.8.cloned.1.call-start = ((), (), s32[]{:S(2)}) async-start(), calls=%async_computation | async-start | bytes 4718592 | tf_op jit(solution)/shard_map/psum | solution.py:144
  10.5 11.3 %collective-permute-start = (bf16[1,32,256]{2,1,0:T(8,128)(2,1)S(1)}, bf16[1,32,256]{2,1,0:T(8,128)(2,1)S(1)}, u32[]{:S(2)}, u32[]{:S(2)}) collective-permute-start(bf16[1,32,256]{2,1,0:T(8,128)(2,1)S(1)} %fusion.39), channel_id=1, source_target_pairs={{0,1},{1,0},{2,3},{3,2},{4,5},{5,4},{6,7},{7,6},{8,9},{9,8},{10,11... | collective-permute-start | bytes 49160 | tf_op jit(solution)/shard_map/ppermute | solution.py:8
  13.4 4.4 %collective-permute-start.3 = (bf16[1,32,256]{2,1,0:T(8,128)(2,1)S(1)}, bf16[1,32,256]{2,1,0:T(8,128)(2,1)S(1)}, u32[]{:S(2)}, u32[]{:S(2)}) collective-permute-start(bf16[1,32,256]{2,1,0:T(8,128)(2,1)S(1)} %fusion.37), channel_id=1, source_target_pairs={{0,1},{1,0},{2,3},{3,2},{4,5},{5,4},{6,7},{7,6},{8,9},{9,8},{10,11... | collective-permute-start | bytes 49160 | tf_op jit(solution)/shard_map/ppermute | solution.py:8
  15.9 3.1 collective-permute-start.4
  18.3 3.4 copy-start.2
  100.7 64.8 %copy-start = (bf16[1,256,9,256]{3,1,2,0:T(8,128)(2,1)}, bf16[1,256,9,256]{3,1,2,0:T(8,128)(2,1)S(1)}, u32[]{:S(2)}) copy-start(bf16[1,256,9,256]{3,1,2,0:T(8,128)(2,1)S(1)} %copy.51) | copy-start | bytes 3538948
  100.7 1.1 copy-start.17
  100.9 1.2 copy-start.24
  101.9 1.0 copy-start.23
  102.8 0.9 copy-start.3
  105.4 1.0 copy-start.22
  105.6 1.0 copy-start.21
  106.3 1.0 copy-start.20
  106.6 1.0 copy-start.19
  107.3 1.0 copy-start.18
  107.6 1.0 copy-start.16
  108.3 1.0 copy-start.15
  108.6 1.0 copy-start.14
  109.3 1.1 copy-start.31
  109.5 1.0 copy-start.27
  109.8 4.0 %copy-start.13 = (bf16[1,16,32,256]{3,2,1,0:T(8,128)(2,1)S(1)}, bf16[1,16,32,256]{3,2,1,0:T(8,128)(2,1)}, u32[]{:S(2)}) copy-start(bf16[1,16,32,256]{3,2,1,0:T(8,128)(2,1)} %get-tuple-element.47) | copy-start | bytes 786436
  110.5 3.6 copy-start.12
  110.6 16.1 %collective-permute-start.1 = (bf16[2,1,16,32,256]{4,3,2,1,0:T(8,128)(2,1)S(1)}, bf16[2,1,16,32,256]{4,3,2,1,0:T(8,128)(2,1)S(1)}, u32[]{:S(2)}, u32[]{:S(2)}) collective-permute-start(bf16[2,1,16,32,256]{4,3,2,1,0:T(8,128)(2,1)S(1)} %pad_maximum_fusion.1), channel_id=1, source_target_pairs={{0,128},{128,256},{256,384},{1,129},{129,257},{257,385},{2,130},{1... | collective-permute-start | bytes 1572872 | tf_op jit(solution)/shard_map/ppermute | solution.py:14
  114.3 1.2 copy-start.6
  115.6 11.1 %copy-start.30 = (bf16[2,1,16,32,256]{4,3,2,1,0:T(8,128)(2,1)S(1)}, bf16[2,1,16,32,256]{4,3,2,1,0:T(8,128)(2,1)}, u32[]{:S(2)}) copy-start(bf16[2,1,16,32,256]{4,3,2,1,0:T(8,128)(2,1)} %param.7) | copy-start | bytes 1572868
  115.8 12.9 %copy-start.25 = (bf16[1,1,16,32,256]{4,3,2,0,1:T(8,128)(2,1)S(1)}, bf16[1,1,16,32,256]{4,3,2,0,1:T(8,128)(2,1)}, u32[]{:S(2)}) copy-start(bf16[1,1,16,32,256]{4,3,2,0,1:T(8,128)(2,1)} %get-tuple-element.12) | copy-start | bytes 786436
  115.8 12.9 %copy-start.26 = (bf16[1,1,16,32,256]{4,3,2,0,1:T(8,128)(2,1)S(1)}, bf16[1,1,16,32,256]{4,3,2,0,1:T(8,128)(2,1)}, u32[]{:S(2)}) copy-start(bf16[1,1,16,32,256]{4,3,2,0,1:T(8,128)(2,1)} %get-tuple-element.14) | copy-start | bytes 786436
  126.8 4.6 %collective-permute-start.2 = (bf16[1,32,256]{2,1,0:T(8,128)(2,1)S(1)}, bf16[1,32,256]{2,1,0:T(8,128)(2,1)S(1)}, u32[]{:S(2)}, u32[]{:S(2)}) collective-permute-start(bf16[1,32,256]{2,1,0:T(8,128)(2,1)S(1)} %fusion.38), channel_id=1, source_target_pairs={{0,1},{1,0},{2,3},{3,2},{4,5},{5,4},{6,7},{7,6},{8,9},{9,8},{10,11... | collective-permute-start | bytes 49160 | tf_op jit(solution)/shard_map/ppermute | solution.py:8
  128.9 27.5 %collective-permute-start.5 = (bf16[4,1,16,32,256]{4,3,2,0,1:T(8,128)(2,1)S(1)}, bf16[4,1,16,32,256]{4,3,2,0,1:T(8,128)(2,1)S(1)}, u32[]{:S(2)}, u32[]{:S(2)}) collective-permute-start(bf16[4,1,16,32,256]{4,3,2,0,1:T(8,128)(2,1)S(1)} %pad_maximum_fusion), channel_id=1, source_target_pairs={{128,0},{256,128},{384,256},{129,1},{257,129},{385,257},{130,2},{2... | collective-permute-start | bytes 3145736 | tf_op jit(solution)/shard_map/ppermute | solution.py:14
  134.0 22.3 %copy-start.29 = (bf16[1,1,16,32,256]{4,3,2,0,1:T(8,128)(2,1)S(1)}, bf16[1,1,16,32,256]{4,3,2,0,1:T(8,128)(2,1)}, u32[]{:S(2)}) copy-start(bf16[1,1,16,32,256]{4,3,2,0,1:T(8,128)(2,1)} %get-tuple-element.16) | copy-start | bytes 786436
  134.0 22.3 %copy-start.32 = (bf16[2,1,16,32,256]{4,3,2,1,0:T(8,128)(2,1)S(1)}, bf16[2,1,16,32,256]{4,3,2,1,0:T(8,128)(2,1)}, u32[]{:S(2)}) copy-start(bf16[2,1,16,32,256]{4,3,2,1,0:T(8,128)(2,1)} %param.8) | copy-start | bytes 1572868
  157.2 4.5 %collective-permute-start.7 = (bf16[1,32,256]{2,1,0:T(8,128)(2,1)S(1)}, bf16[1,32,256]{2,1,0:T(8,128)(2,1)S(1)}, u32[]{:S(2)}, u32[]{:S(2)}) collective-permute-start(bf16[1,32,256]{2,1,0:T(8,128)(2,1)S(1)} %fusion.34), channel_id=1, source_target_pairs={{0,1},{1,0},{2,3},{3,2},{4,5},{5,4},{6,7},{7,6},{8,9},{9,8},{10,11... | collective-permute-start | bytes 49160 | tf_op jit(solution)/shard_map/ppermute | solution.py:8
  159.2 5.3 %collective-permute-start.6 = (bf16[1,32,256]{2,1,0:T(8,128)(2,1)S(1)}, bf16[1,32,256]{2,1,0:T(8,128)(2,1)S(1)}, u32[]{:S(2)}, u32[]{:S(2)}) collective-permute-start(bf16[1,32,256]{2,1,0:T(8,128)(2,1)S(1)} %fusion.35), channel_id=1, source_target_pairs={{0,1},{1,0},{2,3},{3,2},{4,5},{5,4},{6,7},{7,6},{8,9},{9,8},{10,11... | collective-permute-start | bytes 49160 | tf_op jit(solution)/shard_map/ppermute | solution.py:8
  180.1 1.3 copy-start.1
  180.1 2.5 copy-start.11
  181.4 1.5 copy-start.9
  183.2 1.0 copy-start.8
  183.5 1.0 copy-start.10
  184.1 1.0 copy-start.7
  184.5 1.1 copy-start.4
  185.5 0.9 copy-start.28
Sparse Core Ops, SparseCore 0:
  11.7 86.9 all-gather.2
  180.3 199.0 all-reduce.7
where the time goes:
time: 389 us; the launch traced here: 388 us
  waiting for transfers between devices  292 us (75%)
  matrix products  32.2 us (8%)
  local copies, waits for them, and re-layouts  19.9 us (5%)
  starting transfers between devices  18.4 us (5%)
  between operations  15 us (4%)
  other arithmetic  10.5 us (3%)
    psum x1, waiting for transfers between devices, shards(): lax.psum(grad_part(first_terms[0], first_terms[1], channels, height, widt...  192 us
    all_gather x1, waiting for transfers between devices, shards(): full_weight = lax.all_gather(weight_shard, 'dp', axis=0, tiled=True)  67.2 us
    ppermute x2, waiting for transfers between devices, passed_along(): return lax.ppermute(block, axis, route)  32.2 us
    dot_general x36, matrix products, conv_part(): jnp.dot(window_at(extended, row_off, col_off, height, width, amount), wei...  15.3 us
    ppermute x6, starting transfers between devices, from_partner(): lax.ppermute(x, axis, [(i, i ^ 1 << bit) for i in range(lax.axis_size(axi...  12.6 us
    dot_general x18, matrix products, grad_part(): lax.dot_general(window, cot_flat, (((0,), (0,)), ((), ())), preferred_ele...  11.3 us
    unnamed x67, local copies, waits for them, and re-layouts  9.51 us
  transfers between devices with their start and end apart: 10, of which 5 were waited for; matrix products, arithmetic and copies ran while one was open for 7% of the time, Pallas kernels for 0%

commit v1 on v0

v1 whole, which is shorter than its diff:
```python
import functools
import math

import jax
import jax.numpy as jnp
from jax import lax
from jax.experimental import pallas as pl
from jax.experimental.pallas import tpu as pltpu
from jax.sharding import PartitionSpec as P

F32 = jnp.float32
BF16 = jnp.bfloat16
TAPS = 9
TAP_ROWS = 16


class Sems:
    def __init__(self):
        self.count = 0

    def take(self, amount=1):
        first = self.count
        self.count += amount
        return first


def offsets_of(n):
    return sorted(range(1, n), key=lambda i: -min(i, n - i))


def plan(n):
    send, recv, local = Sems(), Sems(), Sems()
    numbers = {}
    for name in ("a2", "y1", "g2", "p2", "yy1", "gc2", "r"):
        numbers["halo_" + name] = (send.take(), recv.take())
    for name in ("p1", "p2", "p2h", "y1", "y1h", "y2", "gc1", "gc2", "gc2h", "fin"):
        numbers["x_" + name] = (send.take(), recv.take())
    for name in ("gather_a", "gather_b", "share", "s1_ring1", "s1_ring2", "s2_ring1", "s2_ring2"):
        numbers[name] = (send.take(n), recv.take(n))
    for name in ("s1_pair", "s2_pair"):
        numbers[name] = (send.take(), recv.take())
    for name in ("w", "y1", "g2", "a2", "a1", "y2", "g1", "fresh0", "fresh1", "top0", "top1", "last1", "o0", "o1", "o2", "o3", "o4", "o5"):
        numbers["local_" + name] = local.take()
    return numbers, send.count, recv.count, local.count


def kernel(
    n, segments, height, width, channels, scale,
    fwd, bwd, fresh, top, w,
    fwd_out, bwd_out, grad_out,
    tf, tb, pp, yy, gc, halo, n2, r1, dx1, out_a, out_b, out_c,
    s_y, s_g, s_a, s_r, s_p, s_y2, s_g2,
    wa, wr, pm, pmt, q1, q2,
    g_1, g_2, pair_send, pair_recv, sum_send, ring1, fold, ring2_send, ring2, res2, fin,
    send, recv, local,
):
    numbers = plan(n)[0]
    pixels = height * width
    half = channels // 2
    block = 2 * n
    seg = lax.axis_index("segment")
    dp = lax.axis_index("dp")
    core = dp % 2
    chip = dp // 2
    py = chip // n
    pz = chip % n
    first = jnp.where(core == 0, py, pz)
    second = jnp.where(core == 0, pz, py)
    last = segments - 1

    def at(f, g):
        y = jnp.where(core == 0, f, g)
        z = jnp.where(core == 0, g, f)
        return (seg, (y * n + z) * 2 + core)

    partner = (seg, dp + 1 - 2 * core)

    def remote(name, src, dst, device, send_slot=0, recv_slot=0):
        s, r = numbers[name]
        return pltpu.make_async_remote_copy(
            src_ref=src,
            dst_ref=dst,
            send_sem=send.at[s + send_slot],
            recv_sem=recv.at[r + recv_slot],
            device_id=device,
            device_id_type=pl.DeviceIdType.MESH,
        )

    def copy(name, src, dst):
        return pltpu.make_async_copy(src, dst, local.at[numbers["local_" + name]])

    def when(flag):
        return pl.when(flag)

    has_next = seg < last
    has_prev = seg > 0
    is_first = seg == 0
    is_last = seg == last

    load_w = copy("w", w, wa.at[second])
    load_y1 = copy("y1", bwd.at[0], tb.at[0])
    load_g2 = copy("g2", bwd.at[3], tb.at[3])
    load_a2 = copy("a2", fwd.at[1], tf.at[1])
    load_a1 = copy("a1", fwd.at[0], tf.at[0])
    load_y2 = copy("y2", bwd.at[1], tb.at[1])
    load_g1 = copy("g1", bwd.at[2], tb.at[2])
    load_fresh = [copy("fresh0", fresh.at[0], pp.at[0]), copy("fresh1", fresh.at[1], pp.at[1])]
    load_top = [
        copy("top0", top.at[0], gc.at[0]),
        copy("top1", top.at[1], gc.at[1]),
        copy("last1", fwd.at[1], yy.at[0]),
    ]

    barrier = pltpu.get_barrier_semaphore()

    def greet(device):
        pl.semaphore_signal(barrier, inc=1, device_id=device, device_id_type=pl.DeviceIdType.MESH)

    for i in offsets_of(n):
        greet(at((first + i) % n, second))
        greet(at(first, (second + i) % n))
    greet(partner)

    @when(has_next)
    def _():
        greet((seg + 1, dp))
        greet((seg + 1, partner[1]))

    @when(has_prev)
    def _():
        greet((seg - 1, dp))
        greet((seg - 1, partner[1]))

    for c in (load_w, load_y1, load_g2, load_a2, load_a1, load_y2, load_g1):
        c.start()

    @when(is_first)
    def _():
        for c in load_fresh:
            c.start()

    @when(is_last)
    def _():
        for c in load_top:
            c.start()

    def natural(k):
        c, f, g, kk = k // half, (k // block) % n, (k // 2) % n, k % 2
        even = f * (4 * n) + g * 4 + kk
        odd = g * (4 * n) + f * 4 + 2 + kk
        return jnp.where(c == 0, even, odd)

    def one_hot(flag):
        return jnp.where(flag, 1.0, 0.0).astype(BF16)

    shape = (channels, channels)
    rows = lax.broadcasted_iota(jnp.int32, shape, 0)
    cols = lax.broadcasted_iota(jnp.int32, shape, 1)
    pm[...] = one_hot(rows == natural(cols))
    pmt[...] = one_hot(natural(rows) == cols)
    shape = (block * TAP_ROWS, block * TAP_ROWS)
    rows = lax.broadcasted_iota(jnp.int32, shape, 0)
    cols = lax.broadcasted_iota(jnp.int32, shape, 1)
    q1[...] = one_hot((rows // block == cols % TAP_ROWS) & (rows % block == cols // TAP_ROWS))
    q2[...] = one_hot((cols // block == rows % TAP_ROWS) & (cols % block == rows // TAP_ROWS))
    fold[...] = jnp.zeros_like(fold)

    def matmul(a, b):
        return jnp.dot(a, b, preferred_element_type=F32)

    def build(dest, tile, edge, permute, relu):
        received = edge[...].astype(F32)
        above = jnp.where(core == 1, received, 0.0).astype(BF16)
        below = jnp.where(core == 0, received, 0.0).astype(BF16)
        whole = jnp.concatenate([above, tile[...].reshape(pixels, channels), below], axis=0)
        value = matmul(whole, pm[...]) if permute else whole.astype(F32)
        if relu:
            value = jnp.maximum(value, 0.0)
        total = pixels + 2 * width
        column = lax.broadcasted_iota(jnp.int32, (total, 1), 0) % width
        full = (height + 2, width, channels)
        dest[1] = value.astype(BF16).reshape(full)
        dest[0] = jnp.where(column == 0, 0.0, pltpu.roll(value, 1, 0)).astype(BF16).reshape(full)
        dest[2] = (
            jnp.where(column == width - 1, 0.0, pltpu.roll(value, total - 1, 0)).astype(BF16).reshape(full)
        )

    def window(s, row_off, col_off):
        return s[col_off, row_off : row_off + height].reshape(pixels, channels)

    def conv(s):
        total = None
        for t in range(TAPS):
            term = matmul(window(s, t // 3, t % 3), wr[t])
            total = term if total is None else total + term
        return total

    def conv_back(s):
        total = None
        for t in range(TAPS):
            term = lax.dot_general(
                window(s, 2 - t // 3, 2 - t % 3), wr[t], (((1,), (1,)), ((), ())), preferred_element_type=F32
            )
            total = term if total is None else total + term
        return total

    def weight_terms(dest, s, cotangent, add):
        flat = cotangent[...].reshape(pixels, channels)
        for t in range(TAPS):
            term = lax.dot_general(
                window(s, t // 3, t % 3), flat, (((0,), (0,)), ((), ())), preferred_element_type=F32
            )
            dest[t] = dest[t] + term if add else term

    def flat32(tile):
        return tile[...].reshape(pixels, channels).astype(F32)

    def as_tile(value):
        return value.astype(BF16).reshape(height, width, channels)

    def cot_rebuilt(cot_first, s_kept, s_cot):
        moved = matmul(cot_first[...].reshape(pixels, channels), pm[...])
        kept = s_kept[1, 1 : 1 + height].reshape(pixels, channels).astype(F32)
        total = moved + jnp.where(kept > 0, conv_back(s_cot), 0.0)
        return as_tile(matmul(total.astype(BF16), pmt[...]))

    load_w.wait()
    load_y1.wait()
    load_g2.wait()
    load_a2.wait()
    neighbours = 2 * (n - 1) + 1 + 2 * has_next.astype(jnp.int32) + 2 * has_prev.astype(jnp.int32)
    pl.semaphore_wait(barrier, neighbours)

    gather_a = [
        remote("gather_a", wa.at[second], wa.at[second], at(first, (second + i) % n), i, second)
        for i in offsets_of(n)
    ]
    for c in gather_a:
        c.start()

    edge_row = jnp.where(core == 0, height - 1, 0)
    halos = [
        remote("halo_y1", tb.at[0, edge_row], halo.at[1], partner),
        remote("halo_g2", tb.at[3, edge_row], halo.at[2], partner),
        remote("halo_a2", tf.at[1, edge_row], halo.at[0], partner),
    ]
    for c in halos:
        c.start()
    halo_fresh = remote("halo_p2", pp.at[1, edge_row], halo.at[3], partner)
    halo_top = [
        remote("halo_yy1", tf.at[1, edge_row], halo.at[4], partner),
        remote("halo_gc2", gc.at[1, edge_row], halo.at[5], partner),
    ]

    ahead = (seg + 1, dp)
    ahead_partner = (seg + 1, partner[1])
    behind = (seg - 1, dp)
    behind_partner = (seg - 1, partner[1])
    x_p1 = remote("x_p1", tf.at[1], pp.at[0], ahead)
    x_p2 = remote("x_p2", n2, pp.at[1], ahead)
    x_p2h = remote("x_p2h", n2.at[edge_row], halo.at[3], ahead_partner)
    x_y2 = remote("x_y2", tb.at[0], yy.at[1], behind)
    x_gc1 = remote("x_gc1", tb.at[3], gc.at[0], behind)
    x_y1 = remote("x_y1", r1, yy.at[0], behind)
    x_y1h = remote("x_y1h", r1.at[edge_row], halo.at[4], behind_partner)
    x_gc2 = remote("x_gc2", dx1, gc.at[1], behind)
    x_gc2h = remote("x_gc2h", dx1.at[edge_row], halo.at[5], behind_partner)
    x_fin = remote("x_fin", res2, fin, behind)

    @when(has_prev)
    def _():
        x_y2.start()
        x_gc1.start()

    @when(has_next)
    def _():
        x_p1.start()

    @when(is_first)
    def _():
        for c in load_fresh:
            c.wait()
        halo_fresh.start()

    @when(is_last)
    def _():
        for c in load_top:
            c.wait()
        for c in halo_top:
            c.start()

    other_half = pl.multiple_of((1 - core) * half, half)
    own_half = pl.multiple_of(core * half, half)
    own_block = pl.multiple_of(first * block, block)

    def scatter(k, g):
        tag = f"s{k + 1}_"
        pair = remote(tag + "pair", pair_send.at[k], pair_recv.at[k], partner)
        sends1 = []
        for i in offsets_of(n):
            peer = (first + i) % n
            rows = pl.ds(pl.multiple_of(peer * block, block), block)
            sends1.append(
                remote(tag + "ring1", sum_send.at[k, :, rows], ring1.at[k, first], at(peer, second), i, first)
            )
        sends2 = []
        for i in offsets_of(n):
            peer = (second + i) % n
            sends2.append(
                remote(tag + "ring2", ring2_send.at[k, peer], ring2.at[k, second], at(first, peer), i, second)
            )

        def stage0():
            pair_send[k] = g[:, pl.ds(other_half, half), :].astype(BF16)
            pair.start()

        def stage1_sum():
            pair.wait_recv()
            sum_send[k] = (g[:, pl.ds(own_half, half), :] + pair_recv[k].astype(F32)).astype(BF16)

        def stage1_send():
            for c in sends1:
                c.start()

        def stage2():
            total = sum_send[k, :, pl.ds(own_block, block), :].astype(F32)
            for i in reversed(offsets_of(n)):
                peer = (first + n - i) % n
                remote(tag + "ring1", ring1.at[k, peer], ring1.at[k, peer], partner, i, peer).wait_recv()
                total = total + ring1[k, peer].astype(F32)
            fold[0:TAPS] = total.astype(BF16)
            sorted_rows = matmul(q2[...], fold[...].reshape(TAP_ROWS * block, channels))
            ring2_send[k] = sorted_rows.astype(BF16).reshape(n, 2, TAP_ROWS, channels)
            for c in sends2:
                c.start()

        def stage3():
            total = ring2_send[k, second].astype(F32)
            for i in reversed(offsets_of(n)):
                peer = (second + n - i) % n
                remote(tag + "ring2", ring2.at[k, peer], ring2.at[k, peer], partner, i, peer).wait_recv()
                total = total + ring2[k, peer].astype(F32)
            return total

        def finish():
            pair.wait_send()
            for c in sends1 + sends2:
                c.wait_send()

        return stage0, stage1_sum, stage1_send, stage2, stage3, finish

    one = scatter(0, g_1)
    two = scatter(1, g_2)

    halos[0].wait_recv()
    build(s_y, tb.at[0], halo.at[1], True, True)
    halos[1].wait_recv()
    build(s_g, tb.at[3], halo.at[2], False, False)

    for i in reversed(offsets_of(n)):
        peer = (second + n - i) % n
        remote("gather_a", wa.at[peer], wa.at[peer], partner, i, peer).wait_recv()
    line = matmul(q1[...], wa[...].reshape(block * TAP_ROWS, channels)).astype(BF16)
    mine = pl.multiple_of(own_half + own_block, block)
    wr[:, pl.ds(mine, block), :] = line[: TAPS * block].reshape(TAPS, block, channels)

    def share(f):
        rows = pl.ds(pl.multiple_of(own_half + f * block, block), block)
        return remote("share", wr.at[:, rows], wr.at[:, rows], partner, f, f)

    mine_rows = pl.ds(mine, block)
    gather_b = [
        remote("gather_b", wr.at[:, mine_rows], wr.at[:, mine_rows], at((first + i) % n, second), i, first)
        for i in offsets_of(n)
    ]
    for c in gather_b:
        c.start()
    share(first).start()

    weight_terms(g_1, s_y, tb.at[3], False)
    halos[2].wait_recv()
    build(s_a, tf.at[1], halo.at[0], True, True)

    @when(is_last)
    def _():
        weight_terms(g_1, s_a, gc.at[1], True)

    one[0]()

    for i in reversed(offsets_of(n)):
        peer = (first + n - i) % n
        rows = pl.ds(pl.multiple_of(own_half + peer * block, block), block)
        remote("gather_b", wr.at[:, rows], wr.at[:, rows], partner, i, peer).wait_recv()
        share(peer).start()
    one[1]()
    for f in range(n):
        rows = pl.ds(pl.multiple_of(other_half + f * block, block), block)
        remote("share", wr.at[:, rows], wr.at[:, rows], partner, f, f).wait_recv()
    one[2]()

    load_y2.wait()
    r1[...] = as_tile(flat32(tb.at[1]) - conv(s_y))
    halo_r = remote("halo_r", r1.at[edge_row], halo.at[6], partner)

    @when(has_prev)
    def _():
        halo_r.start()
        x_y1h.start()
        x_y1.start()

    load_g1.wait()
    dx1[...] = cot_rebuilt(tb.at[2], s_y, s_g)

    @when(has_prev)
    def _():
        x_gc2h.start()
        x_gc2.start()
        halo_r.wait_recv()
        build(s_r, r1, halo.at[6], True, True)
        weight_terms(g_2, s_r, dx1, False)
        two[0]()

    load_a1.wait()
    n2[...] = as_tile(flat32(tf.at[0]) + conv(s_a))

    @when(has_next)
    def _():
        x_p2h.start()
        x_p2.start()

    @when(is_last)
    def _():
        yy[1] = n2[...]

    @when(has_prev)
    def _():
        two[1]()
        two[2]()

    def ready(local_flag, names):
        @when(jnp.logical_not(local_flag))
        def _():
            for name, ref in names:
                remote(name, ref, ref, partner).wait_recv()

    @when(is_last)
    def _():
        for c in halo_top:
            c.wait_recv()

    @when(is_first)
    def _():
        halo_fresh.wait_recv()

    ready(is_last, [("x_y1h", halo.at[4]), ("x_y1", yy.at[0]), ("x_y2", yy.at[1])])
    build(s_y2, yy.at[0], halo.at[4], True, True)
    out_b[...] = as_tile(flat32(yy.at[1]) - conv(s_y2))
    out = [copy("o0", out_b, bwd_out.at[0]), copy("o1", yy.at[0], bwd_out.at[1])]

    one[3]()

    ready(is_first, [("x_p2h", halo.at[3]), ("x_p2", pp.at[1]), ("x_p1", pp.at[0])])
    build(s_p, pp.at[1], halo.at[3], True, True)
    out_a[...] = as_tile(flat32(pp.at[0]) + conv(s_p))
    out += [copy("o2", pp.at[1], fwd_out.at[0]), copy("o3", out_a, fwd_out.at[1])]
    for c in out:
        c.start()

    @when(has_prev)
    def _():
        two[3]()

    ready(is_last, [("x_gc2h", halo.at[5]), ("x_gc2", gc.at[1]), ("x_gc1", gc.at[0])])
    build(s_g2, gc.at[1], halo.at[5], False, False)
    out_c[...] = cot_rebuilt(gc.at[0], s_y2, s_g2)
    more = [copy("o4", gc.at[1], bwd_out.at[2]), copy("o5", out_c, bwd_out.at[3])]
    for c in more:
        c.start()
    total = one[4]()
    grad_out[...] = total

    @when(has_prev)
    def _():
        res2[...] = two[4]()
        x_fin.start()

    @when(has_next)
    def _():
        x_fin.wait_recv()
        grad_out[...] = grad_out[...] + fin[...]

    grad_out[...] = grad_out[...] * scale

    for c in gather_a + gather_b + halos:
        c.wait_send()
    for f in range(n):
        share(f).wait_send()
    one[5]()

    @when(has_prev)
    def _():
        for c in (x_y2, x_gc1, x_y1, x_y1h, x_gc2, x_gc2h, x_fin, halo_r):
            c.wait_send()
        two[5]()

    @when(has_next)
    def _():
        for c in (x_p1, x_p2, x_p2h):
            c.wait_send()

    @when(is_first)
    def _():
        halo_fresh.wait_send()

    @when(is_last)
    def _():
        for c in halo_top:
            c.wait_send()

    for c in out + more:
        c.wait()


def fused(n, segments, scale, fwd, bwd, fresh, top, w):
    height, width, channels = fwd.shape[1:]
    tile = (height, width, channels)
    shifted = (3, height + 2, width, channels)
    half = channels // 2
    block = 2 * n
    _, n_send, n_recv, n_local = plan(n)
    square = (channels, channels)
    mixed = (block * TAP_ROWS, block * TAP_ROWS)
    v = pltpu.VMEM
    scratch = [
        v((2, *tile), BF16),
        v((4, *tile), BF16),
        v((2, *tile), BF16),
        v((2, *tile), BF16),
        v((2, *tile), BF16),
        v((7, width, channels), BF16),
        v(tile, BF16),
        v(tile, BF16),
        v(tile, BF16),
        v(tile, BF16),
        v(tile, BF16),
        v(tile, BF16),
        *[v(shifted, BF16)] * 7,
        v((n, 2, TAP_ROWS, channels), BF16),
        v((TAPS, channels, channels), BF16),
        v(square, BF16),
        v(square, BF16),
        v(mixed, BF16),
        v(mixed, BF16),
        v((TAPS, channels, channels), F32),
        v((TAPS, channels, channels), F32),
        v((2, TAPS, half, channels), BF16),
        v((2, TAPS, half, channels), BF16),
        v((2, TAPS, half, channels), BF16),
        v((2, n, TAPS, block, channels), BF16),
        v((TAP_ROWS, block, channels), BF16),
        v((2, n, 2, TAP_ROWS, channels), BF16),
        v((2, n, 2, TAP_ROWS, channels), BF16),
        v((2, TAP_ROWS, channels), F32),
        v((2, TAP_ROWS, channels), F32),
        pltpu.SemaphoreType.DMA((n_send,)),
        pltpu.SemaphoreType.DMA((n_recv,)),
        pltpu.SemaphoreType.DMA((n_local,)),
    ]
    return pl.pallas_call(
        functools.partial(kernel, n, segments, height, width, channels, scale),
        out_shape=(
            jax.ShapeDtypeStruct((2, *tile), BF16),
            jax.ShapeDtypeStruct((4, *tile), BF16),
            jax.ShapeDtypeStruct((2, TAP_ROWS, channels), F32),
        ),
        in_specs=[pl.BlockSpec(memory_space=pl.ANY)] * 5,
        out_specs=(
            pl.BlockSpec(memory_space=pl.ANY),
            pl.BlockSpec(memory_space=pl.ANY),
            pl.BlockSpec(memory_space=pltpu.VMEM),
        ),
        scratch_shapes=scratch,
        compiler_params=pltpu.CompilerParams(collective_id=0, has_side_effects=True),
        name="coupling",
    )(fwd, bwd, fresh, top, w)


def shards(segments, tiles, fwd_in, bwd_in, fresh, top_cot, conv_weight):
    height, width, channels = fwd_in.shape[3:]
    n = math.isqrt(tiles // 2)
    scale = (2.0 * tiles * height * width) ** (-0.5)
    weight = jnp.pad(conv_weight[0], ((0, 0), (0, TAP_ROWS - TAPS), (0, 0)))
    forward, message, grad = fused(
        n, segments, scale, fwd_in[:, 0, 0], bwd_in[:, 0, 0], fresh[:, 0], top_cot[:, 0], weight
    )
    return forward[:, None, None], message[:, None, None], grad[None, :, :TAPS]


def solution(mesh):
    segments = mesh.shape["segment"]
    tiles = mesh.shape["dp"]
    streams = P(None, "segment", "dp", None, None, None)
    halves = P(None, "dp", None, None, None)
    weights = P("segment", "dp", None, None)
    return jax.shard_map(
        functools.partial(shards, segments, tiles),
        mesh=mesh,
        in_specs=(streams, streams, halves, halves, weights),
        out_specs=(streams, streams, weights),
        check_vma=False,
    )
```

time: 389 us -> 63.3 us (0.16)
  the two profiles are of different devices: /device:TPU:28 before, /device:TPU:2 now
where the time goes in v1:
time: 63.3 us; the launch traced here: 63.1 us
  Pallas kernels  56.8 us (90%)
  local copies, waits for them, and re-layouts  5.63 us (9%)
  between operations  0.65 us (1%)
    pallas_call x1, Pallas kernels, fused(): pl.pallas_call(functools.partial(kernel, n, segments, height, width, chan...  56.8 us
    unnamed x6, local copies, waits for them, and re-layouts  4.17 us

profile of v1, /device:TPU:2, one launch (start us, length us, event | category | flops | bytes accessed | tf_op | source)
XLA Modules:
  0.0 63.1 jit_solution(15715023458341002271)
XLA Ops:
  0.6 0.7 %copy.13 = bf16[1,2,9,256]{3,2,1,0:T(8,128)(2,1)S(1)} copy(bf16[1,2,9,256]{3,1,2,0:T(2,128)(2,1)} %param.9) | data formatting | bytes 18432 | tf_op args[4]
  1.3 0.6 pad.4.w
  1.9 56.8 %coupling.1 = (bf16[2,16,32,256]{3,2,1,0:T(8,128)(2,1)}, bf16[4,16,32,256]{3,2,1,0:T(8,128)(2,1)}, f32[2,16,256]{2,1,0:T(8,128)}) custom-call(bf16[2,16,32,256]{3,2,1,0:T(8,128)(2,1)} %bitcast.17, bf16[4,16,32,256]{3,2,1,0:T(8,128)(2,1)} %bitcast.15, bf16[2,16,32,256]{3,2,1,0:T(8,128)(2,1)} %bitcast.18, bf16[2,16,32,256]{3,2,1,0:T(8,128)(2,1)} %bitcast.19, ...), custom_call_target="tpu_custom_call" | custom-call | tf_op jit(solution)/shard_map/coupling/pallas_call | solution.py:569
  58.8 0.0 copy-start
  58.8 0.8 %slice_bitcast_fusion = f32[1,2,9,256]{3,2,1,0:T(8,128)S(1)} fusion(f32[2,16,256]{2,1,0:T(8,128)} %get-tuple-element.8), kind=kLoop, calls=%fused_computation | loop fusion | bytes 36864 | tf_op jit(solution)/shard_map/broadcast_in_dim | solution.py:596
  59.6 0.6 copy.11
  60.2 1.9 %copy.16 = bf16[2,1,1,16,32,256]{5,4,3,2,1,0:T(8,128)(2,1)} copy(bf16[2,1,1,16,32,256]{5,4,3,2,1,0:T(8,128)(2,1)} %bitcast.20) | data formatting | bytes 1048576
  62.1 0.0 copy-done
  62.1 1.0 %copy.17 = bf16[4,1,1,16,32,256]{5,4,3,2,1,0:T(8,128)(2,1)} copy(bf16[4,1,1,16,32,256]{5,4,3,2,1,0:T(8,128)(2,1)S(1)} %bitcast.16) | data formatting | bytes 2097152
Async XLA Ops:
  58.8 3.4 %copy-start = (bf16[4,16,32,256]{3,2,1,0:T(8,128)(2,1)S(1)}, bf16[4,16,32,256]{3,2,1,0:T(8,128)(2,1)}, u32[]{:S(2)}) copy-start(bf16[4,16,32,256]{3,2,1,0:T(8,128)(2,1)} %get-tuple-element.7) | copy-start | bytes 3145732

commit v2 on v1

v2 whole, which is shorter than its diff:
```python
import functools
import math

import jax
import jax.numpy as jnp
from jax import lax
from jax.experimental import pallas as pl
from jax.experimental.pallas import tpu as pltpu
from jax.sharding import PartitionSpec as P

F32 = jnp.float32
BF16 = jnp.bfloat16
TAPS = 9
TAP_ROWS = 16
GROUPS = (((0, 9),), ((0, 3), (3, 6), (6, 9)))
SPLIT = 5


class Sems:
    def __init__(self):
        self.count = 0

    def take(self, amount=1):
        first = self.count
        self.count += amount
        return first


def offsets_of(n):
    return sorted(range(1, n), key=lambda i: -min(i, n - i))


def plan(n):
    send, recv, local = Sems(), Sems(), Sems()
    sends = ("gather_a", "gather_b", "share", "halo", "edge", "x_back", "x_back_row", "x_ahead", "x_ahead_row", "x_fin")
    sends = {name: send.take() for name in sends + ("s1_ring1", "s2_ring1", "s1_ring2", "s2_ring2")}
    recvs = ("gather_a", "share", "h_yg", "h_a2", "h_r", "h_p", "h_y", "h_g", "x_pp", "x_yy", "x_gc", "x_fin")
    recvs = {name: recv.take() for name in recvs + ("s1_ring1", "s2_ring1", "s1_ring2", "s2_ring2", "s1_relay", "s2_relay")}
    recvs["gather_b"] = recv.take(n)
    for name, parts in (("s1_pair", len(GROUPS[0])), ("s2_pair", len(GROUPS[1]))):
        sends[name] = send.take()
        recvs[name] = recv.take(parts)
    locals_ = {name: local.take() for name in ("w", "y1", "g2", "a2", "a1", "mid", "fresh", "top", "last1", "fo", "bo")}
    return sends, recvs, locals_, send.count, recv.count, local.count


def kernel(
    n, segments, height, width, channels, scale,
    fwd, bwd, fresh, top, w,
    fwd_out, bwd_out, grad_out,
    tf, tb, pp, yy, gc, halo, n2, r1, dx1, out_a, out_b, out_c,
    s_y, s_g, s_a, s_r, s_p, s_y2, s_g2,
    wa, wr, pm, pmt, q2, rows_f32,
    g_1, g_2, pair_send, pair_recv, sum_send, relayed, ring1, fold, ring2_send, ring2, res2, fin,
    send, recv, local,
):
    sends, recvs, locals_ = plan(n)[:3]
    far = n // 2 - 1
    pixels = height * width
    half = channels // 2
    block = 2 * n
    seg = lax.axis_index("segment")
    dp = lax.axis_index("dp")
    core = dp % 2
    chip = dp // 2
    py = chip // n
    pz = chip % n
    first = jnp.where(core == 0, py, pz)
    second = jnp.where(core == 0, pz, py)
    last = segments - 1

    def at(f, g):
        y = jnp.where(core == 0, f, g)
        z = jnp.where(core == 0, g, f)
        return (seg, (y * n + z) * 2 + core)

    partner = (seg, dp + 1 - 2 * core)

    def remote(send_name, recv_name, src, dst, device, recv_slot=0):
        return pltpu.make_async_remote_copy(
            src_ref=src,
            dst_ref=dst,
            send_sem=send.at[sends[send_name]],
            recv_sem=recv.at[recvs[recv_name] + recv_slot],
            device_id=device,
            device_id_type=pl.DeviceIdType.MESH,
        )

    def arrived(recv_name, ref, recv_slot=0):
        remote("halo", recv_name, ref, ref, partner, recv_slot).wait_recv()

    def sent(send_name, ref):
        remote(send_name, "share", ref, ref, partner).wait_send()

    def copy(name, src, dst):
        return pltpu.make_async_copy(src, dst, local.at[locals_[name]])

    def when(flag):
        return pl.when(flag)

    has_next = seg < last
    has_prev = seg > 0
    is_first = seg == 0
    is_last = seg == last

    load_w = copy("w", w, wa.at[second])
    load_y1 = copy("y1", bwd.at[0], tb.at[0])
    load_g2 = copy("g2", bwd.at[3], tb.at[3])
    load_a2 = copy("a2", fwd.at[1], tf.at[1])
    load_a1 = copy("a1", fwd.at[0], tf.at[0])
    load_mid = copy("mid", bwd.at[1:3], tb.at[1:3])
    load_fresh = copy("fresh", fresh, pp)
    load_top = copy("top", top, gc)
    load_last = copy("last1", fwd.at[1], yy.at[0])

    barrier = pltpu.get_barrier_semaphore()

    def greet(device):
        pl.semaphore_signal(barrier, inc=1, device_id=device, device_id_type=pl.DeviceIdType.MESH)

    for i in offsets_of(n):
        greet(at((first + i) % n, second))
        greet(at(first, (second + i) % n))
    greet(partner)

    @when(has_next)
    def _():
        greet((seg + 1, dp))
        greet((seg + 1, partner[1]))

    @when(has_prev)
    def _():
        greet((seg - 1, dp))
        greet((seg - 1, partner[1]))

    for c in (load_w, load_y1, load_g2, load_a2, load_a1, load_mid):
        c.start()

    @when(is_first)
    def _():
        load_fresh.start()

    @when(is_last)
    def _():
        load_top.start()
        load_last.start()

    def natural(k):
        c, f, g, kk = k // half, (k // block) % n, (k // 2) % n, k % 2
        even = f * (4 * n) + g * 4 + kk
        odd = g * (4 * n) + f * 4 + 2 + kk
        return jnp.where(c == 0, even, odd)

    def one_hot(flag):
        return jnp.where(flag, 1.0, 0.0).astype(BF16)

    shape = (channels, channels)
    rows = lax.broadcasted_iota(jnp.int32, shape, 0)
    cols = lax.broadcasted_iota(jnp.int32, shape, 1)
    pm[...] = one_hot(rows == natural(cols))
    pmt[...] = one_hot(natural(rows) == cols)
    shape = (block * TAP_ROWS, block * TAP_ROWS)
    rows = lax.broadcasted_iota(jnp.int32, shape, 0)
    cols = lax.broadcasted_iota(jnp.int32, shape, 1)
    q2[...] = one_hot(
        (rows // (2 * TAP_ROWS) == (cols % block) // 2)
        & ((rows // 2) % TAP_ROWS == cols // block)
        & (rows % 2 == cols % 2)
    )
    fold[...] = jnp.zeros_like(fold)

    def matmul(a, b):
        return jnp.dot(a, b, preferred_element_type=F32)

    def build(dest, tile, edge, permute, relu):
        received = edge[...].astype(F32)
        above = jnp.where(core == 1, received, 0.0).astype(BF16)
        below = jnp.where(core == 0, received, 0.0).astype(BF16)
        whole = jnp.concatenate([above, tile[...].reshape(pixels, channels), below], axis=0)
        value = matmul(whole, pm[...]) if permute else whole.astype(F32)
        if relu:
            value = jnp.maximum(value, 0.0)
        total = pixels + 2 * width
        column = lax.broadcasted_iota(jnp.int32, (total, 1), 0) % width
        full = (height + 2, width, channels)
        dest[1] = value.astype(BF16).reshape(full)
        dest[0] = jnp.where(column == 0, 0.0, pltpu.roll(value, 1, 0)).astype(BF16).reshape(full)
        dest[2] = (
            jnp.where(column == width - 1, 0.0, pltpu.roll(value, total - 1, 0)).astype(BF16).reshape(full)
        )

    def window(s, row_off, col_off):
        return s[col_off, row_off : row_off + height].reshape(pixels, channels)

    def conv(s):
        total = None
        for t in range(TAPS):
            term = matmul(window(s, t // 3, t % 3), wr[t])
            total = term if total is None else total + term
        return total

    def conv_back(s):
        total = None
        for t in range(TAPS):
            term = lax.dot_general(
                window(s, 2 - t // 3, 2 - t % 3), wr[t], (((1,), (1,)), ((), ())), preferred_element_type=F32
            )
            total = term if total is None else total + term
        return total

    def weight_terms(dest, s, cotangent, add, t):
        flat = cotangent[...].reshape(pixels, channels)
        term = lax.dot_general(
            window(s, t // 3, t % 3), flat, (((0,), (0,)), ((), ())), preferred_element_type=F32
        )
        dest[t] = dest[t] + term if add else term

    def flat32(tile):
        return tile[...].reshape(pixels, channels).astype(F32)

    def as_tile(value):
        return value.astype(BF16).reshape(height, width, channels)

    def cot_rebuilt(cot_first, s_kept, s_cot):
        moved = matmul(cot_first[...].reshape(pixels, channels), pm[...])
        kept = s_kept[1, 1 : 1 + height].reshape(pixels, channels).astype(F32)
        total = moved + jnp.where(kept > 0, conv_back(s_cot), 0.0)
        return as_tile(matmul(total.astype(BF16), pmt[...]))

    load_w.wait()
    load_y1.wait()
    load_g2.wait()
    load_a2.wait()
    neighbours = 2 * (n - 1) + 1 + 2 * has_next.astype(jnp.int32) + 2 * has_prev.astype(jnp.int32)
    pl.semaphore_wait(barrier, neighbours)

    for i in offsets_of(n):
        remote("gather_a", "gather_a", wa.at[second], wa.at[second], at(first, (second + i) % n)).start()

    edge_row = jnp.where(core == 0, height - 1, 0)
    remote("halo", "h_yg", tb.at[0, edge_row], halo.at[1], partner).start()
    remote("halo", "h_yg", tb.at[3, edge_row], halo.at[2], partner).start()
    remote("halo", "h_a2", tf.at[1, edge_row], halo.at[0], partner).start()

    ahead = (seg + 1, dp)
    ahead_partner = (seg + 1, partner[1])
    behind = (seg - 1, dp)
    behind_partner = (seg - 1, partner[1])

    @when(has_prev)
    def _():
        remote("x_back", "x_yy", tb.at[0], yy.at[1], behind).start()
        remote("x_back", "x_gc", tb.at[3], gc.at[0], behind).start()

    @when(has_next)
    def _():
        remote("x_ahead", "x_pp", tf.at[1], pp.at[0], ahead).start()

    @when(is_first)
    def _():
        load_fresh.wait()
        remote("edge", "h_p", pp.at[1, edge_row], halo.at[3], partner).start()

    @when(is_last)
    def _():
        load_top.wait()
        load_last.wait()
        remote("edge", "h_y", tf.at[1, edge_row], halo.at[4], partner).start()
        remote("edge", "h_g", gc.at[1, edge_row], halo.at[5], partner).start()

    other_half = pl.multiple_of((1 - core) * half, half)
    own_half = pl.multiple_of(core * half, half)
    own_block = pl.multiple_of(first * block, block)

    def block_rows(f):
        return pl.ds(pl.multiple_of(f * block, block), block)

    def scatter(k, g):
        tag = f"s{k + 1}_"
        relay_taps = ((slice(0, SPLIT), 1), (slice(SPLIT, TAPS), -1))

        def pair_start(part):
            lo, hi = GROUPS[k][part]
            pair_send[k, lo:hi] = g[lo:hi, pl.ds(other_half, half), :].astype(BF16)
            src, dst = pair_send.at[k, lo:hi], pair_recv.at[k, lo:hi]
            remote(tag + "pair", tag + "pair", src, dst, partner, part).start()

        def pair_sum():
            for part, (lo, hi) in enumerate(GROUPS[k]):
                arrived(tag + "pair", pair_recv.at[k, lo:hi], part)
                own = g[lo:hi, pl.ds(own_half, half), :]
                sum_send[k, lo:hi] = (own + pair_recv[k, lo:hi].astype(F32)).astype(BF16)

        def ring_send(i):
            peer = (first + n + i) % n
            src = sum_send.at[k, :, block_rows(peer)]
            remote(tag + "ring1", tag + "ring1", src, ring1.at[k, first], at(peer, second)).start()

        def ring1_near():
            if far > 0:
                for taps, way in relay_taps:
                    src = sum_send.at[k, taps, block_rows((first + n // 2) % n)]
                    dst = relayed.at[k, taps]
                    device = at((first + n + way) % n, second)
                    remote(tag + "ring1", tag + "relay", src, dst, device).start()
                for i in range(far - 1, 0, -1):
                    ring_send(i)
                    ring_send(-i)
            else:
                ring_send(1)

        def ring1_far():
            if far > 0:
                arrived(tag + "relay", relayed.at[k])
                for taps, way in relay_taps:
                    rows = block_rows((first + n + way * far) % n)
                    own = sum_send[k, taps, rows, :].astype(F32)
                    sum_send[k, taps, rows, :] = (own + relayed[k, taps].astype(F32)).astype(BF16)
                ring_send(far)
                ring_send(-far)

        def ring2_start():
            total = sum_send[k, :, pl.ds(own_block, block), :].astype(F32)
            near = [i for i in range(1, n) if far == 0 or i != n // 2]
            arrived(tag + "ring1", ring1.at[k, 0 : len(near)])
            for i in near:
                total = total + ring1[k, (first + i) % n].astype(F32)
            fold[0:TAPS] = total.astype(BF16)
            sorted_rows = matmul(q2[...], fold[...].reshape(TAP_ROWS * block, channels))
            ring2_send[k] = sorted_rows.astype(BF16).reshape(n, 2 * TAP_ROWS, channels)
            for i in offsets_of(n):
                peer = (second + i) % n
                src, dst = ring2_send.at[k, peer], ring2.at[k, second]
                remote(tag + "ring2", tag + "ring2", src, dst, at(first, peer)).start()

        def ring2_sum():
            total = ring2_send[k, second].astype(F32)
            arrived(tag + "ring2", ring2.at[k, 0 : n - 1])
            for i in range(1, n):
                total = total + ring2[k, (second + i) % n].astype(F32)
            return total[0 : 2 * TAPS + 6]

        def finish():
            sent(tag + "pair", pair_send.at[k])
            sent(tag + "ring1", sum_send.at[k, :, 0 : (n - 1) * block])
            sent(tag + "ring2", ring2_send.at[k, 0 : n - 1])

        return pair_start, pair_sum, ring1_near, ring1_far, ring2_start, ring2_sum, finish

    one_pair, one_sum, one_near, one_far, one_ring2, one_total, one_finish = scatter(0, g_1)
    two_pair, two_sum, two_near, two_far, two_ring2, two_total, two_finish = scatter(1, g_2)

    arrived("h_yg", halo.at[1:3])
    build(s_y, tb.at[0], halo.at[1], True, True)
    build(s_g, tb.at[3], halo.at[2], False, False)

    def weight_rows(c, f):
        return pl.ds(pl.multiple_of(c * half + f * block, block), block)

    arrived("gather_a", wa.at[0 : n - 1])
    for g in range(n):
        for t in range(TAPS):
            rows_f32[t * block + 2 * g : t * block + 2 * g + 2, :] = wa[g, t].astype(F32)
    mine = weight_rows(core, first)
    wr[:, mine, :] = rows_f32[...].astype(BF16).reshape(TAPS, block, channels)

    def weight_send(src, way, taps, slot):
        ref = wr.at[taps, weight_rows(core, src)]
        remote("gather_b", "gather_b", ref, ref, at((first + n + way) % n, second), slot).start()

    def share(f):
        ref = wr.at[:, weight_rows(core, f)]
        remote("share", "share", ref, ref, partner).start()

    def weights_from(f):
        arrived("gather_b", wr.at[:, weight_rows(core, f)], f)

    every = slice(0, TAPS)
    reach = range(far, 0, -1) if far > 0 else [1]
    for i in reach:
        weight_send(first, i, every, first)
        if far > 0:
            weight_send(first, -i, every, first)
    share(first)

    for t in range(TAPS):
        weight_terms(g_1, s_y, tb.at[3], False, t)
    arrived("h_a2", halo.at[0])
    build(s_a, tf.at[1], halo.at[0], True, True)

    @when(is_last)
    def _():
        for t in range(TAPS):
            weight_terms(g_1, s_a, gc.at[1], True, t)

    one_pair(0)

    opposite = (first + n // 2) % n
    if far > 0:
        for way in (1, -1):
            origin = (first + n + way * far) % n
            weights_from(origin)
            taps = slice(0, SPLIT) if way > 0 else slice(SPLIT, TAPS)
            receiver = (first + n - way) % n
            slot = origin if way > 0 else receiver
            weight_send(origin, -way, taps, slot)
            share(origin)
        for i in range(1, far):
            for way in (1, -1):
                origin = (first + n + way * i) % n
                weights_from(origin)
                share(origin)
        arrived("gather_b", wr.at[0:SPLIT, weight_rows(core, opposite)], opposite)
        arrived("gather_b", wr.at[SPLIT:TAPS, weight_rows(core, opposite)], first)
    else:
        weights_from(opposite)
    share(opposite)
    one_sum()
    arrived("share", wr.at[:, pl.ds(other_half, half)])
    one_near()

    load_mid.wait()
    r1[...] = as_tile(flat32(tb.at[1]) - conv(s_y))

    @when(has_prev)
    def _():
        remote("x_back_row", "h_r", r1.at[edge_row], halo.at[6], partner).start()
        remote("x_back_row", "h_y", r1.at[edge_row], halo.at[4], behind_partner).start()
        remote("x_back", "x_yy", r1, yy.at[0], behind).start()

    dx1[...] = cot_rebuilt(tb.at[2], s_y, s_g)

    @when(has_prev)
    def _():
        remote("x_back_row", "h_g", dx1.at[edge_row], halo.at[5], behind_partner).start()
        remote("x_back", "x_gc", dx1, gc.at[1], behind).start()
        arrived("h_r", halo.at[6])
        build(s_r, r1, halo.at[6], True, True)
        for part, (lo, hi) in enumerate(GROUPS[1]):
            for t in range(lo, hi):
                weight_terms(g_2, s_r, dx1, False, t)
            two_pair(part)

    one_far()
    load_a1.wait()
    n2[...] = as_tile(flat32(tf.at[0]) + conv(s_a))

    @when(has_next)
    def _():
        remote("x_ahead_row", "h_p", n2.at[edge_row], halo.at[3], ahead_partner).start()
        remote("x_ahead", "x_pp", n2, pp.at[1], ahead).start()

    @when(is_last)
    def _():
        yy[1] = n2[...]

    @when(has_prev)
    def _():
        two_sum()
        two_near()
        two_far()

    arrived("h_y", halo.at[4])

    @when(has_next)
    def _():
        arrived("x_yy", yy)

    build(s_y2, yy.at[0], halo.at[4], True, True)
    out_b[...] = as_tile(flat32(yy.at[1]) - conv(s_y2))
    copy("bo", out_b, bwd_out.at[0]).start()
    copy("bo", yy.at[0], bwd_out.at[1]).start()

    one_ring2()

    arrived("h_p", halo.at[3])

    @when(has_prev)
    def _():
        arrived("x_pp", pp)

    build(s_p, pp.at[1], halo.at[3], True, True)
    out_a[...] = as_tile(flat32(pp.at[0]) + conv(s_p))
    copy("fo", pp.at[1], fwd_out.at[0]).start()
    copy("fo", out_a, fwd_out.at[1]).start()

    @when(has_prev)
    def _():
        two_ring2()

    arrived("h_g", halo.at[5])

    @when(has_next)
    def _():
        arrived("x_gc", gc)

    build(s_g2, gc.at[1], halo.at[5], False, False)
    out_c[...] = cot_rebuilt(gc.at[0], s_y2, s_g2)
    copy("bo", gc.at[1], bwd_out.at[2]).start()
    copy("bo", out_c, bwd_out.at[3]).start()
    rows_f32[0 : 2 * TAPS + 6, :] = one_total()

    @when(has_prev)
    def _():
        res2[...] = two_total()
        remote("x_fin", "x_fin", res2, fin, behind).start()

    @when(has_next)
    def _():
        arrived("x_fin", fin)
        rows_f32[0 : 2 * TAPS + 6, :] = rows_f32[0 : 2 * TAPS + 6, :] + fin[...]

    for t in range(TAPS):
        grad_out[t] = rows_f32[2 * t : 2 * t + 2, :] * scale

    sent("gather_a", wa.at[0 : n - 1])
    sent("gather_b", wr.at[:, 0 : (n - 1) * block])
    sent("share", wr.at[:, pl.ds(other_half, half)])
    sent("halo", halo.at[0:3])
    one_finish()

    @when(has_prev)
    def _():
        sent("x_back", tb)
        sent("x_back_row", halo.at[0:3])
        sent("x_fin", fin)
        two_finish()

    @when(has_next)
    def _():
        sent("x_ahead", tf)
        sent("x_ahead_row", halo.at[0])

    @when(is_first)
    def _():
        sent("edge", halo.at[0])

    @when(is_last)
    def _():
        sent("edge", halo.at[0:2])

    copy("fo", fwd_out, fwd_out).wait()
    copy("bo", bwd_out, bwd_out).wait()


def fused(n, segments, scale, fwd, bwd, fresh, top, w):
    height, width, channels = fwd.shape[1:]
    tile = (height, width, channels)
    shifted = (3, height + 2, width, channels)
    half = channels // 2
    block = 2 * n
    n_send, n_recv, n_local = plan(n)[3:]
    square = (channels, channels)
    mixed = (block * TAP_ROWS, block * TAP_ROWS)
    v = pltpu.VMEM
    scratch = [
        v((2, *tile), BF16),
        v((4, *tile), BF16),
        v((2, *tile), BF16),
        v((2, *tile), BF16),
        v((2, *tile), BF16),
        v((7, width, channels), BF16),
        v(tile, BF16),
        v(tile, BF16),
        v(tile, BF16),
        v(tile, BF16),
        v(tile, BF16),
        v(tile, BF16),
        *[v(shifted, BF16)] * 7,
        v((n, TAPS, 2, channels), BF16),
        v((TAPS, channels, channels), BF16),
        v(square, BF16),
        v(square, BF16),
        v(mixed, BF16),
        v((max(TAPS * block, 2 * TAPS + 6), channels), F32),
        v((TAPS, channels, channels), F32),
        v((TAPS, channels, channels), F32),
        v((2, TAPS, half, channels), BF16),
        v((2, TAPS, half, channels), BF16),
        v((2, TAPS, half, channels), BF16),
        v((2, TAPS, block, channels), BF16),
        v((2, n, TAPS, block, channels), BF16),
        v((TAP_ROWS, block, channels), BF16),
        v((2, n, 2 * TAP_ROWS, channels), BF16),
        v((2, n, 2 * TAP_ROWS, channels), BF16),
        v((2 * TAPS + 6, channels), F32),
        v((2 * TAPS + 6, channels), F32),
        pltpu.SemaphoreType.DMA((n_send,)),
        pltpu.SemaphoreType.DMA((n_recv,)),
        pltpu.SemaphoreType.DMA((n_local,)),
    ]
    return pl.pallas_call(
        functools.partial(kernel, n, segments, height, width, channels, scale),
        out_shape=(
            jax.ShapeDtypeStruct((2, *tile), BF16),
            jax.ShapeDtypeStruct((4, *tile), BF16),
            jax.ShapeDtypeStruct((TAPS, 2, channels), F32),
        ),
        in_specs=[pl.BlockSpec(memory_space=pltpu.HBM)] * 5,
        out_specs=(
            pl.BlockSpec(memory_space=pl.ANY),
            pl.BlockSpec(memory_space=pl.ANY),
            pl.BlockSpec(memory_space=pltpu.VMEM),
        ),
        scratch_shapes=scratch,
        compiler_params=pltpu.CompilerParams(collective_id=0, has_side_effects=True, vmem_limit_bytes=44 << 20),
        name="coupling",
    )(fwd, bwd, fresh, top, w)


def shards(segments, tiles, fwd_in, bwd_in, fresh, top_cot, conv_weight):
    height, width, channels = fwd_in.shape[3:]
    n = math.isqrt(tiles // 2)
    scale = (2.0 * tiles * height * width) ** (-0.5)
    weight = conv_weight[0].transpose(1, 0, 2)
    forward, message, grad = fused(
        n, segments, scale, fwd_in[:, 0, 0], bwd_in[:, 0, 0], fresh[:, 0], top_cot[:, 0], weight
    )
    return forward[:, None, None], message[:, None, None], grad.transpose(1, 0, 2)[None]


def solution(mesh):
    segments = mesh.shape["segment"]
    tiles = mesh.shape["dp"]
    streams = P(None, "segment", "dp", None, None, None)
    halves = P(None, "dp", None, None, None)
    weights = P("segment", "dp", None, None)
    return jax.shard_map(
        functools.partial(shards, segments, tiles),
        mesh=mesh,
        in_specs=(streams, streams, halves, halves, weights),
        out_specs=(streams, streams, weights),
        check_vma=False,
    )
```

time: 63.3 us -> 62.8 us (level)
  the two profiles are of different devices: /device:TPU:2 before, /device:TPU:10 now
where the time goes in v2:
time: 62.8 us; the launch traced here: 62.4 us
  Pallas kernels  54.4 us (87%)
  local copies, waits for them, and re-layouts  7.41 us (12%)
  between operations  0.65 us (1%)
    pallas_call x1, Pallas kernels, fused(): pl.pallas_call(functools.partial(kernel, n, segments, height, width, chan...  54.4 us
    unnamed x13, local copies, waits for them, and re-layouts  7.41 us

profile of v2, /device:TPU:10, one launch (start us, length us, event | category | flops | bytes accessed | tf_op | source)
XLA Modules:
  0.0 62.4 jit_solution(16725985882342144006)
XLA Ops:
  0.6 0.0 copy-start.4
  0.6 0.7 %copy-done.4 = bf16[1,2,9,256]{3,1,2,0:T(2,128)(2,1)S(1)} copy-done((bf16[1,2,9,256]{3,1,2,0:T(2,128)(2,1)S(1)}, bf16[1,2,9,256]{3,1,2,0:T(2,128)(2,1)}, u32[]{:S(2)}) %copy-start.4) | copy-done | bytes 9240
  1.3 0.0 copy-start
  1.3 1.2 %copy-done = bf16[4,1,1,16,32,256]{5,4,3,2,1,0:T(8,128)(2,1)S(1)} copy-done((bf16[4,1,1,16,32,256]{5,4,3,2,1,0:T(8,128)(2,1)S(1)}, bf16[4,1,1,16,32,256]{5,4,3,2,1,0:T(8,128)(2,1)}, u32[]{:S(2)}) %copy-start) | copy-done | bytes 1048600
  2.6 0.0 copy-start.1
  2.6 1.0 %copy-done.1 = bf16[2,1,1,16,32,256]{5,4,3,2,1,0:T(8,128)(2,1)S(1)} copy-done((bf16[2,1,1,16,32,256]{5,4,3,2,1,0:T(8,128)(2,1)S(1)}, bf16[2,1,1,16,32,256]{5,4,3,2,1,0:T(8,128)(2,1)}, u32[]{:S(2)}) %copy-start.1) | copy-done | bytes 524312
  3.6 0.0 copy-start.2
  3.6 1.0 %copy-done.2 = bf16[2,1,16,32,256]{4,3,2,1,0:T(8,128)(2,1)S(1)} copy-done((bf16[2,1,16,32,256]{4,3,2,1,0:T(8,128)(2,1)S(1)}, bf16[2,1,16,32,256]{4,3,2,1,0:T(8,128)(2,1)}, u32[]{:S(2)}) %copy-start.2) | copy-done | bytes 524312
  4.6 0.0 copy-start.3
  4.6 1.0 %copy-done.3 = bf16[2,1,16,32,256]{4,3,2,1,0:T(8,128)(2,1)S(1)} copy-done((bf16[2,1,16,32,256]{4,3,2,1,0:T(8,128)(2,1)S(1)}, bf16[2,1,16,32,256]{4,3,2,1,0:T(8,128)(2,1)}, u32[]{:S(2)}) %copy-start.3) | copy-done | bytes 524312
  5.7 54.4 %coupling.1 = (bf16[2,16,32,256]{3,2,1,0:T(8,128)(2,1)S(1)}, bf16[4,16,32,256]{3,2,1,0:T(8,128)(2,1)S(1)}, f32[9,2,256]{2,1,0:T(2,128)S(1)}) custom-call(bf16[2,16,32,256]{3,2,1,0:T(8,128)(2,1)S(1)} %bitcast.18, bf16[4,16,32,256]{3,2,1,0:T(8,128)(2,1)S(1)} %bitcast.16, bf16[2,16,32,256]{3,2,1,0:T(8,128)(2,1)S(1)} %bitcast.19, ...), custom_call_target="tpu_custom_call" | custom-call | tf_op jit(solution)/shard_map/coupling/pallas_call | solution.py:592
  60.1 0.8 %copy.13 = bf16[2,1,1,16,32,256]{5,4,3,2,1,0:T(8,128)(2,1)} copy(bf16[2,1,1,16,32,256]{5,4,3,2,1,0:T(8,128)(2,1)S(1)} %bitcast.21) | data formatting | bytes 1048576
  60.9 1.0 %copy.14 = bf16[4,1,1,16,32,256]{5,4,3,2,1,0:T(8,128)(2,1)} copy(bf16[4,1,1,16,32,256]{5,4,3,2,1,0:T(8,128)(2,1)S(1)} %bitcast.17) | data formatting | bytes 2097152
  61.8 0.6 copy.15
Async XLA Ops:
  0.6 0.7 %copy-start.4 = (bf16[1,2,9,256]{3,1,2,0:T(2,128)(2,1)S(1)}, bf16[1,2,9,256]{3,1,2,0:T(2,128)(2,1)}, u32[]{:S(2)}) copy-start(bf16[1,2,9,256]{3,1,2,0:T(2,128)(2,1)} %param.9) | copy-start | bytes 27652
  1.3 1.2 %copy-start = (bf16[4,1,1,16,32,256]{5,4,3,2,1,0:T(8,128)(2,1)S(1)}, bf16[4,1,1,16,32,256]{5,4,3,2,1,0:T(8,128)(2,1)}, u32[]{:S(2)}) copy-start(bf16[4,1,1,16,32,256]{5,4,3,2,1,0:T(8,128)(2,1)} %param.6) | copy-start | bytes 3145732
  2.6 1.0 %copy-start.1 = (bf16[2,1,1,16,32,256]{5,4,3,2,1,0:T(8,128)(2,1)S(1)}, bf16[2,1,1,16,32,256]{5,4,3,2,1,0:T(8,128)(2,1)}, u32[]{:S(2)}) copy-start(bf16[2,1,1,16,32,256]{5,4,3,2,1,0:T(8,128)(2,1)} %param.5) | copy-start | bytes 1572868
  3.6 1.0 %copy-start.2 = (bf16[2,1,16,32,256]{4,3,2,1,0:T(8,128)(2,1)S(1)}, bf16[2,1,16,32,256]{4,3,2,1,0:T(8,128)(2,1)}, u32[]{:S(2)}) copy-start(bf16[2,1,16,32,256]{4,3,2,1,0:T(8,128)(2,1)} %param.7) | copy-start | bytes 1572868
  4.6 1.0 %copy-start.3 = (bf16[2,1,16,32,256]{4,3,2,1,0:T(8,128)(2,1)S(1)}, bf16[2,1,16,32,256]{4,3,2,1,0:T(8,128)(2,1)}, u32[]{:S(2)}) copy-start(bf16[2,1,16,32,256]{4,3,2,1,0:T(8,128)(2,1)} %param.8) | copy-start | bytes 1572868

commit v3 on v2

--- a/solution.py
+++ b/solution.py
@@ -434,6 +434,11 @@
     def _():
         remote("x_back_row", "h_g", dx1.at[edge_row], halo.at[5], behind_partner).start()
         remote("x_back", "x_gc", dx1, gc.at[1], behind).start()
+
+    one_far()
+
+    @when(has_prev)
+    def _():
         arrived("h_r", halo.at[6])
         build(s_r, r1, halo.at[6], True, True)
         for part, (lo, hi) in enumerate(GROUPS[1]):
@@ -441,7 +446,6 @@
                 weight_terms(g_2, s_r, dx1, False, t)
             two_pair(part)
 
-    one_far()
     load_a1.wait()
     n2[...] = as_tile(flat32(tf.at[0]) + conv(s_a))
 
@@ -605,7 +609,30 @@
         scratch_shapes=scratch,
         compiler_params=pltpu.CompilerParams(collective_id=0, has_side_effects=True, vmem_limit_bytes=44 << 20),
         name="coupling",
-    )(fwd, bwd, fresh, top, w)
+    )(*[pltpu.with_memory_space_constraint(x, pltpu.HBM) for x in (fwd, bwd, fresh, top, w)])
+
+
+def place_kernel(a, b, c, a_out, b_out, c_out, sems):
+    copies = [
+        pltpu.make_async_copy(src, dst, sems.at[i])
+        for i, (src, dst) in enumerate(((b, b_out), (a, a_out), (c, c_out)))
+    ]
+    for c in copies:
+        c.start()
+    for c in copies:
+        c.wait()
+
+
+def placed(arrays):
+    return pl.pallas_call(
+        place_kernel,
+        out_shape=tuple(jax.ShapeDtypeStruct(x.shape, x.dtype) for x in arrays),
+        in_specs=[pl.BlockSpec(memory_space=pl.ANY)] * 3,
+        out_specs=(pl.BlockSpec(memory_space=pl.ANY),) * 3,
+        scratch_shapes=[pltpu.SemaphoreType.DMA((3,))],
+        compiler_params=pltpu.CompilerParams(vmem_limit_bytes=8 << 20),
+        name="place",
+    )(*arrays)
 
 
 def shards(segments, tiles, fwd_in, bwd_in, fresh, top_cot, conv_weight):
@@ -613,9 +640,10 @@
     n = math.isqrt(tiles // 2)
     scale = (2.0 * tiles * height * width) ** (-0.5)
     weight = conv_weight[0].transpose(1, 0, 2)
-    forward, message, grad = fused(
+    results = fused(
         n, segments, scale, fwd_in[:, 0, 0], bwd_in[:, 0, 0], fresh[:, 0], top_cot[:, 0], weight
     )
+    forward, message, grad = placed(results)
     return forward[:, None, None], message[:, None, None], grad.transpose(1, 0, 2)[None]
 
 

time: 62.8 us -> 57.5 us (0.916)
  the two profiles are of different devices: /device:TPU:10 before, /device:TPU:8 now
where the time goes in v3:
time: 57.5 us; the launch traced here: 57.4 us
  Pallas kernels  56.8 us (99%)
  between operations  0.64 us (1%)
    pallas_call x1, Pallas kernels, fused(): pl.pallas_call(functools.partial(kernel, n, segments, height, width, chan...  55.6 us
    pallas_call x1, Pallas kernels, placed(): pl.pallas_call(place_kernel, out_shape=tuple((jax.ShapeDtypeStruct(x.shap...  1.17 us

profile of v3, /device:TPU:8, one launch (start us, length us, event | category | flops | bytes accessed | tf_op | source)
XLA Modules:
  0.0 57.4 jit_solution(17627521070373309297)
XLA Ops:
  0.6 55.6 %coupling.1 = (bf16[2,16,32,256]{3,2,1,0:T(8,128)(2,1)S(1)}, bf16[4,16,32,256]{3,2,1,0:T(8,128)(2,1)S(1)}, f32[9,2,256]{2,1,0:T(2,128)S(1)}) custom-call(bf16[2,16,32,256]{3,2,1,0:T(8,128)(2,1)} %bitcast.17, bf16[4,16,32,256]{3,2,1,0:T(8,128)(2,1)} %bitcast.16, bf16[2,16,32,256]{3,2,1,0:T(8,128)(2,1)} %bitcast.18, bf16[2,16,32,256]{3,2,1,0:T(8,128)(2,1)} %bitcast.19, ...), custom_call_target="tpu_custom_call" | custom-call | tf_op jit(solution)/shard_map/coupling/pallas_call | solution.py:596
  56.2 1.2 %place.1 = (bf16[2,16,32,256]{3,2,1,0:T(8,128)(2,1)}, bf16[4,16,32,256]{3,2,1,0:T(8,128)(2,1)}, f32[9,2,256]{2,1,0:T(2,128)}) custom-call(bf16[2,16,32,256]{3,2,1,0:T(8,128)(2,1)S(1)} %get-tuple-element.9.a, bf16[4,16,32,256]{3,2,1,0:T(8,128)(2,1)S(1)} %get-tuple-element.10.b, f32[9,2,256]{2,1,0:T(2,128)S(1)} %get-tuple-element.11.c), custom_call_target="tpu_custom_call" | custom-call | tf_op jit(solution)/shard_map/place/pallas_call | solution.py:627

commit v4 on v3

--- a/solution.py
+++ b/solution.py
@@ -35,7 +35,7 @@
     sends = ("gather_a", "gather_b", "share", "halo", "edge", "x_back", "x_back_row", "x_ahead", "x_ahead_row", "x_fin")
     sends = {name: send.take() for name in sends + ("s1_ring1", "s2_ring1", "s1_ring2", "s2_ring2")}
     recvs = ("gather_a", "share", "h_yg", "h_a2", "h_r", "h_p", "h_y", "h_g", "x_pp", "x_yy", "x_gc", "x_fin")
-    recvs = {name: recv.take() for name in recvs + ("s1_ring1", "s2_ring1", "s1_ring2", "s2_ring2", "s1_relay", "s2_relay")}
+    recvs = {name: recv.take() for name in recvs + ("s1_ring1", "s2_ring1", "s1_ring2", "s2_ring2", "s1_full", "s2_full", "s1_part", "s2_part")}
     recvs["gather_b"] = recv.take(n)
     for name, parts in (("s1_pair", len(GROUPS[0])), ("s2_pair", len(GROUPS[1]))):
         sends[name] = send.take()
@@ -51,11 +51,12 @@
     tf, tb, pp, yy, gc, halo, n2, r1, dx1, out_a, out_b, out_c,
     s_y, s_g, s_a, s_r, s_p, s_y2, s_g2,
     wa, wr, pm, pmt, q2, rows_f32,
-    g_1, g_2, pair_send, pair_recv, sum_send, relayed, ring1, fold, ring2_send, ring2, res2, fin,
+    g_1, g_2, pair_send, pair_recv, sum_send, full, part_, ring1, fold, ring2_send, ring2, res2, fin,
     send, recv, local,
 ):
     sends, recvs, locals_ = plan(n)[:3]
-    far = n // 2 - 1
+    hop = n // 4
+    beyond = range(hop + 1, n // 2) if hop > 0 else range(0)
     pixels = height * width
     half = channels // 2
     block = 2 * n
@@ -277,7 +278,7 @@
 
     def scatter(k, g):
         tag = f"s{k + 1}_"
-        relay_taps = ((slice(0, SPLIT), 1), (slice(SPLIT, TAPS), -1))
+        ways = ((1, slice(0, SPLIT)), (-1, slice(SPLIT, TAPS)))
 
         def pair_start(part):
             lo, hi = GROUPS[k][part]
@@ -291,40 +292,53 @@
                 own = g[lo:hi, pl.ds(own_half, half), :]
                 sum_send[k, lo:hi] = (own + pair_recv[k, lo:hi].astype(F32)).astype(BF16)
 
-        def ring_send(i):
-            peer = (first + n + i) % n
-            src = sum_send.at[k, :, block_rows(peer)]
-            remote(tag + "ring1", tag + "ring1", src, ring1.at[k, first], at(peer, second)).start()
+        def away(i):
+            return (first + n + i) % n
+
+        def ring_send(way, i):
+            slot = 2 * (i - 1) + (0 if way > 0 else 1)
+            src = sum_send.at[k, :, block_rows(away(way * i))]
+            remote(tag + "ring1", tag + "ring1", src, ring1.at[k, slot], at(away(way * i), second)).start()
 
         def ring1_near():
-            if far > 0:
-                for taps, way in relay_taps:
-                    src = sum_send.at[k, taps, block_rows((first + n // 2) % n)]
-                    dst = relayed.at[k, taps]
-                    device = at((first + n + way) % n, second)
-                    remote(tag + "ring1", tag + "relay", src, dst, device).start()
-                for i in range(far - 1, 0, -1):
-                    ring_send(i)
-                    ring_send(-i)
-            else:
-                ring_send(1)
+            if hop == 0:
+                ring_send(1, 1)
+                return
+            for way, taps in ways:
+                for e in beyond:
+                    src = sum_send.at[k, :, block_rows(away(way * e))]
+                    dst = full.at[k, 2 * (e - hop - 1) + (0 if way > 0 else 1)]
+                    remote(tag + "ring1", tag + "full", src, dst, at(away(way * (e - hop)), second)).start()
+            for way, taps in ways:
+                src = sum_send.at[k, taps, block_rows(away(n // 2))]
+                device = at(away(way * (n // 2 - hop)), second)
+                remote(tag + "ring1", tag + "part", src, part_.at[k, taps], device).start()
+            for i in range(1, hop):
+                for way, _ in ways:
+                    ring_send(way, i)
 
         def ring1_far():
-            if far > 0:
-                arrived(tag + "relay", relayed.at[k])
-                for taps, way in relay_taps:
-                    rows = block_rows((first + n + way * far) % n)
-                    own = sum_send[k, taps, rows, :].astype(F32)
-                    sum_send[k, taps, rows, :] = (own + relayed[k, taps].astype(F32)).astype(BF16)
-                ring_send(far)
-                ring_send(-far)
+            if hop == 0:
+                return
+            if len(beyond) > 0:
+                arrived(tag + "full", full.at[k])
+            arrived(tag + "part", part_.at[k])
+            for way, taps in ways:
+                rows = block_rows(away(way * hop))
+                total = sum_send[k, :, rows, :].astype(F32)
+                for e in beyond:
+                    total = total + full[k, 2 * (e - hop - 1) + (0 if way > 0 else 1)].astype(F32)
+                sum_send[k, :, rows, :] = total.astype(BF16)
+                own = total[taps] + part_[k, taps].astype(F32)
+                sum_send[k, taps, rows, :] = own.astype(BF16)
+                ring_send(way, hop)
 
         def ring2_start():
             total = sum_send[k, :, pl.ds(own_block, block), :].astype(F32)
-            near = [i for i in range(1, n) if far == 0 or i != n // 2]
-            arrived(tag + "ring1", ring1.at[k, 0 : len(near)])
-            for i in near:
-                total = total + ring1[k, (first + i) % n].astype(F32)
+            slots = 2 * hop if hop > 0 else 1
+            arrived(tag + "ring1", ring1.at[k])
+            for i in range(slots):
+                total = total + ring1[k, i].astype(F32)
             fold[0:TAPS] = total.astype(BF16)
             sorted_rows = matmul(q2[...], fold[...].reshape(TAP_ROWS * block, channels))
             ring2_send[k] = sorted_rows.astype(BF16).reshape(n, 2 * TAP_ROWS, channels)
@@ -376,10 +390,9 @@
         arrived("gather_b", wr.at[:, weight_rows(core, f)], f)
 
     every = slice(0, TAPS)
-    reach = range(far, 0, -1) if far > 0 else [1]
-    for i in reach:
+    for i in range(max(hop, 1), 0, -1):
         weight_send(first, i, every, first)
-        if far > 0:
+        if hop > 0:
             weight_send(first, -i, every, first)
     share(first)
 
@@ -396,18 +409,20 @@
     one_pair(0)
 
     opposite = (first + n // 2) % n
-    if far > 0:
+    if hop > 0:
         for way in (1, -1):
-            origin = (first + n + way * far) % n
+            origin = (first + n - way * hop) % n
             weights_from(origin)
+            for e in beyond:
+                weight_send(origin, way * (e - hop), every, origin)
             taps = slice(0, SPLIT) if way > 0 else slice(SPLIT, TAPS)
-            receiver = (first + n - way) % n
+            receiver = (first + n + way * (n // 2 - hop)) % n
             slot = origin if way > 0 else receiver
-            weight_send(origin, -way, taps, slot)
+            weight_send(origin, way * (n // 2 - hop), taps, slot)
             share(origin)
-        for i in range(1, far):
+        for i in [*range(1, hop), *beyond]:
             for way in (1, -1):
-                origin = (first + n + way * i) % n
+                origin = (first + n - way * i) % n
                 weights_from(origin)
                 share(origin)
         arrived("gather_b", wr.at[0:SPLIT, weight_rows(core, opposite)], opposite)
@@ -582,8 +597,9 @@
         v((2, TAPS, half, channels), BF16),
         v((2, TAPS, half, channels), BF16),
         v((2, TAPS, half, channels), BF16),
+        v((2, 2 * max(n // 2 - 1 - n // 4, 1), TAPS, block, channels), BF16),
         v((2, TAPS, block, channels), BF16),
-        v((2, n, TAPS, block, channels), BF16),
+        v((2, max(2 * (n // 4), 1), TAPS, block, channels), BF16),
         v((TAP_ROWS, block, channels), BF16),
         v((2, n, 2 * TAP_ROWS, channels), BF16),
         v((2, n, 2 * TAP_ROWS, channels), BF16),

time: 57.5 us -> 59.4 us (1.033)
  the two profiles are of different devices: /device:TPU:8 before, /device:TPU:2 now
where the time goes in v4:
time: 59.4 us; the launch traced here: 59.2 us
  Pallas kernels  58.6 us (99%)
  between operations  0.64 us (1%)
    pallas_call x1, Pallas kernels, fused(): pl.pallas_call(functools.partial(kernel, n, segments, height, width, chan...  57.4 us

profile of v4, /device:TPU:2, one launch (start us, length us, event | category | flops | bytes accessed | tf_op | source)
XLA Modules:
  0.0 59.2 jit_solution(11719171927527736530)
XLA Ops:
  0.6 57.4 %coupling.1 = (bf16[2,16,32,256]{3,2,1,0:T(8,128)(2,1)S(1)}, bf16[4,16,32,256]{3,2,1,0:T(8,128)(2,1)S(1)}, f32[9,2,256]{2,1,0:T(2,128)S(1)}) custom-call(bf16[2,16,32,256]{3,2,1,0:T(8,128)(2,1)} %bitcast.17, bf16[4,16,32,256]{3,2,1,0:T(8,128)(2,1)} %bitcast.16, bf16[2,16,32,256]{3,2,1,0:T(8,128)(2,1)} %bitcast.18, bf16[2,16,32,256]{3,2,1,0:T(8,128)(2,1)} %bitcast.19, ...), custom_call_target="tpu_custom_call" | custom-call | tf_op jit(solution)/shard_map/coupling/pallas_call | solution.py:612
  58.1 1.2 %place.1 = (bf16[2,16,32,256]{3,2,1,0:T(8,128)(2,1)}, bf16[4,16,32,256]{3,2,1,0:T(8,128)(2,1)}, f32[9,2,256]{2,1,0:T(2,128)}) custom-call(bf16[2,16,32,256]{3,2,1,0:T(8,128)(2,1)S(1)} %get-tuple-element.9.a, bf16[4,16,32,256]{3,2,1,0:T(8,128)(2,1)S(1)} %get-tuple-element.10.b, f32[9,2,256]{2,1,0:T(2,128)S(1)} %get-tuple-element.11.c), custom_call_target="tpu_custom_call" | custom-call | tf_op jit(solution)/shard_map/place/pallas_call | solution.py:643

commit v5 on v3

--- a/solution.py
+++ b/solution.py
@@ -296,8 +296,10 @@
             src = sum_send.at[k, :, block_rows(peer)]
             remote(tag + "ring1", tag + "ring1", src, ring1.at[k, first], at(peer, second)).start()
 
+        relay = k == 1 and far > 0
+
         def ring1_near():
-            if far > 0:
+            if relay:
                 for taps, way in relay_taps:
                     src = sum_send.at[k, taps, block_rows((first + n // 2) % n)]
                     dst = relayed.at[k, taps]
@@ -307,10 +309,11 @@
                     ring_send(i)
                     ring_send(-i)
             else:
-                ring_send(1)
+                for i in offsets_of(n):
+                    ring_send(i)
 
         def ring1_far():
-            if far > 0:
+            if relay:
                 arrived(tag + "relay", relayed.at[k])
                 for taps, way in relay_taps:
                     rows = block_rows((first + n + way * far) % n)
@@ -321,7 +324,7 @@
 
         def ring2_start():
             total = sum_send[k, :, pl.ds(own_block, block), :].astype(F32)
-            near = [i for i in range(1, n) if far == 0 or i != n // 2]
+            near = [i for i in range(1, n) if not relay or i != n // 2]
             arrived(tag + "ring1", ring1.at[k, 0 : len(near)])
             for i in near:
                 total = total + ring1[k, (first + i) % n].astype(F32)
@@ -347,7 +350,7 @@
 
         return pair_start, pair_sum, ring1_near, ring1_far, ring2_start, ring2_sum, finish
 
-    one_pair, one_sum, one_near, one_far, one_ring2, one_total, one_finish = scatter(0, g_1)
+    one_pair, one_sum, one_near, _, one_ring2, one_total, one_finish = scatter(0, g_1)
     two_pair, two_sum, two_near, two_far, two_ring2, two_total, two_finish = scatter(1, g_2)
 
     arrived("h_yg", halo.at[1:3])
@@ -416,8 +419,8 @@
         weights_from(opposite)
     share(opposite)
     one_sum()
+    one_near()
     arrived("share", wr.at[:, pl.ds(other_half, half)])
-    one_near()
 
     load_mid.wait()
     r1[...] = as_tile(flat32(tb.at[1]) - conv(s_y))
@@ -435,10 +438,6 @@
         remote("x_back_row", "h_g", dx1.at[edge_row], halo.at[5], behind_partner).start()
         remote("x_back", "x_gc", dx1, gc.at[1], behind).start()
 
-    one_far()
-
-    @when(has_prev)
-    def _():
         arrived("h_r", halo.at[6])
         build(s_r, r1, halo.at[6], True, True)
         for part, (lo, hi) in enumerate(GROUPS[1]):

time: 57.5 us -> 56.7 us (0.986)
  the two profiles are of different devices: /device:TPU:8 before, /device:TPU:2 now
where the time goes in v5:
time: 56.7 us; the launch traced here: 56.5 us
  Pallas kernels  55.9 us (99%)
  between operations  0.64 us (1%)
    pallas_call x1, Pallas kernels, fused(): pl.pallas_call(functools.partial(kernel, n, segments, height, width, chan...  54.7 us
    pallas_call x1, Pallas kernels, placed(): pl.pallas_call(place_kernel, out_shape=tuple((jax.ShapeDtypeStruct(x.shap...  1.17 us

profile of v5, /device:TPU:2, one launch (start us, length us, event | category | flops | bytes accessed | tf_op | source)
XLA Modules:
  0.0 56.5 jit_solution(6440903464660523375)
XLA Ops:
  0.6 54.7 %coupling.1 = (bf16[2,16,32,256]{3,2,1,0:T(8,128)(2,1)S(1)}, bf16[4,16,32,256]{3,2,1,0:T(8,128)(2,1)S(1)}, f32[9,2,256]{2,1,0:T(2,128)S(1)}) custom-call(bf16[2,16,32,256]{3,2,1,0:T(8,128)(2,1)} %bitcast.17, bf16[4,16,32,256]{3,2,1,0:T(8,128)(2,1)} %bitcast.16, bf16[2,16,32,256]{3,2,1,0:T(8,128)(2,1)} %bitcast.18, bf16[2,16,32,256]{3,2,1,0:T(8,128)(2,1)} %bitcast.19, ...), custom_call_target="tpu_custom_call" | custom-call | tf_op jit(solution)/shard_map/coupling/pallas_call | solution.py:595
  55.3 1.2 %place.1 = (bf16[2,16,32,256]{3,2,1,0:T(8,128)(2,1)}, bf16[4,16,32,256]{3,2,1,0:T(8,128)(2,1)}, f32[9,2,256]{2,1,0:T(2,128)}) custom-call(bf16[2,16,32,256]{3,2,1,0:T(8,128)(2,1)S(1)} %get-tuple-element.9.a, bf16[4,16,32,256]{3,2,1,0:T(8,128)(2,1)S(1)} %get-tuple-element.10.b, f32[9,2,256]{2,1,0:T(2,128)S(1)} %get-tuple-element.11.c), custom_call_target="tpu_custom_call" | custom-call | tf_op jit(solution)/shard_map/place/pallas_call | solution.py:626

commit v6 on v5

--- a/solution.py
+++ b/solution.py
@@ -461,6 +461,11 @@
     def _():
         two_sum()
         two_near()
+
+    one_ring2()
+
+    @when(has_prev)
+    def _():
         two_far()
 
     arrived("h_y", halo.at[4])
@@ -473,8 +478,6 @@
     out_b[...] = as_tile(flat32(yy.at[1]) - conv(s_y2))
     copy("bo", out_b, bwd_out.at[0]).start()
     copy("bo", yy.at[0], bwd_out.at[1]).start()
-
-    one_ring2()
 
     arrived("h_p", halo.at[3])
 

time: 56.7 us -> 56.1 us (0.989)
  Pallas kernels: 55.9 us -> 55.3 us
where the time goes in v6:
time: 56.1 us; the launch traced here: 56 us
  Pallas kernels  55.3 us (99%)
  between operations  0.64 us (1%)
    pallas_call x1, Pallas kernels, fused(): pl.pallas_call(functools.partial(kernel, n, segments, height, width, chan...  54.1 us
    pallas_call x1, Pallas kernels, placed(): pl.pallas_call(place_kernel, out_shape=tuple((jax.ShapeDtypeStruct(x.shap...  1.17 us

profile of v6, /device:TPU:2, one launch (start us, length us, event | category | flops | bytes accessed | tf_op | source)
XLA Modules:
  0.0 56.0 jit_solution(7908380834350830733)
XLA Ops:
  0.6 54.1 %coupling.1 = (bf16[2,16,32,256]{3,2,1,0:T(8,128)(2,1)S(1)}, bf16[4,16,32,256]{3,2,1,0:T(8,128)(2,1)S(1)}, f32[9,2,256]{2,1,0:T(2,128)S(1)}) custom-call(bf16[2,16,32,256]{3,2,1,0:T(8,128)(2,1)} %bitcast.17, bf16[4,16,32,256]{3,2,1,0:T(8,128)(2,1)} %bitcast.16, bf16[2,16,32,256]{3,2,1,0:T(8,128)(2,1)} %bitcast.18, bf16[2,16,32,256]{3,2,1,0:T(8,128)(2,1)} %bitcast.19, ...), custom_call_target="tpu_custom_call" | custom-call | tf_op jit(solution)/shard_map/coupling/pallas_call | solution.py:598
  54.8 1.2 %place.1 = (bf16[2,16,32,256]{3,2,1,0:T(8,128)(2,1)}, bf16[4,16,32,256]{3,2,1,0:T(8,128)(2,1)}, f32[9,2,256]{2,1,0:T(2,128)}) custom-call(bf16[2,16,32,256]{3,2,1,0:T(8,128)(2,1)S(1)} %get-tuple-element.9.a, bf16[4,16,32,256]{3,2,1,0:T(8,128)(2,1)S(1)} %get-tuple-element.10.b, f32[9,2,256]{2,1,0:T(2,128)S(1)} %get-tuple-element.11.c), custom_call_target="tpu_custom_call" | custom-call | tf_op jit(solution)/shard_map/place/pallas_call | solution.py:629
